TPU v7x, 32 devices: a whole 2x2x4 slice. The times are simulated.
32 devices in a mesh: gx: 2 (over y), gy: 4 (over x, core), gz: 4 (over z).
Axes of the slice: x: 2, y: 2, z: 4, core: 2. Of those that a mesh axis runs over, the one named last changes fastest.
Arguments:
- fluid_state: float32 [4, 32, 64, 512], P(None, 'gx', 'gy', 'gz'), may hold values from -6 to 6
- shell_disp: float32 [3, 32768], P(None, ('gy', 'gz')), may hold values from -6 to 6
- quad_weights: float32 [32, 32, 64], P(('gx', 'gy', 'gz')), may hold values from 0.25 to 1
- quad_elements: int32 [32, 32, 64], P(('gx', 'gy', 'gz')), may hold values from 0 to 32767
- owner_cells: int32 [32, 32, 64], P(('gx', 'gy', 'gz')), may hold values from 0 to 32767
- owner_counts: int32 [32, 32], P(('gx', 'gy', 'gz')), may hold values from 0 to 64, as said below
Outputs:
- fluid_out: float32 [4, 32, 64, 512], P(None, 'gx', 'gy', 'gz')
- shell_out: float32 [3, 32768], P(None, ('gy', 'gz'))
Inputs may be any that keep to these rules, and one draw needn't show every extreme that they name: `owner_counts`: some owner has 64 live records from every sender; some owner has none from some sender.
All inputs are finite; a program needn't handle non-finite values.
Results may differ from a plain program's by a relative error of at most 0.000023.
Values sent between devices are 32-bit elements; how exact they have to be, the bound alone decides.
A program may use at most 128 MiB of HBM per device.

v0:
```python
import functools

import jax
import jax.numpy as jnp
from jax import lax
from jax.experimental import pallas as pl
from jax.experimental.pallas import tpu as pltpu
from jax.sharding import PartitionSpec as P

ITERS = 2

advection = 0.2
penalty = 0.5
relaxation = 0.05
AXES = ("gx", "gy", "gz")
MESH = pl.DeviceIdType.MESH
F32 = jnp.float32
BF16 = jnp.bfloat16


class Place:
    def __init__(self, sizes):
        self.nx, self.ny, self.nz = sizes
        self.plane = self.nx * self.ny
        self.x, self.y, self.z = (lax.axis_index(a) for a in AXES)
        self.p = self.x * self.ny + self.y

    def plane_peer(self, d):
        p = lax.rem(self.p + d, self.plane)
        return p, (lax.div(p, self.ny), lax.rem(p, self.ny), self.z)

    def line_peer(self, d):
        z = lax.rem(self.z + d, self.nz)
        return z, (self.x, self.y, z)

    def greet(self):
        sem = pltpu.get_barrier_semaphore()
        for d in range(1, self.plane):
            pl.semaphore_signal(sem, inc=1, device_id=self.plane_peer(d)[1], device_id_type=MESH)
        for d in range(1, self.nz):
            pl.semaphore_signal(sem, inc=1, device_id=self.line_peer(d)[1], device_id_type=MESH)
        for dx in range(1, self.nx):
            for d in range(1, self.nz):
                pl.semaphore_signal(sem, inc=1, device_id=self.side_peer(dx, d)[1], device_id_type=MESH)

    def meet(self):
        pl.semaphore_wait(pltpu.get_barrier_semaphore(), self.plane - 1 + self.nx * (self.nz - 1))

    def side_peer(self, dx, d):
        x, z = lax.rem(self.x + dx, self.nx), lax.rem(self.z + d, self.nz)
        return z, (x, self.y, z)


def send(src, dst, sems, k, device):
    return pltpu.make_async_remote_copy(
        src_ref=src, dst_ref=dst, send_sem=sems.at[0, k], recv_sem=sems.at[1, k],
        device_id=device, device_id_type=MESH,
    )


def start_all(copies):
    for c in copies:
        c.start()
    return copies


def wait_all(copies):
    for c in copies:
        c.wait()


class Halo:
    def __init__(self, here, count, device_of, srcs, dsts, sems):
        self.has = (here > 0, here < count - 1)
        self.copies = []
        for s in (0, 1):
            there = jnp.clip(here + (2 * s - 1), 0, count - 1)
            self.copies.append(send(srcs[s], dsts[1 - s], sems, s, device_of(there)))

    def start(self):
        for s in (0, 1):
            @pl.when(self.has[s])
            def _():
                self.copies[s].start()

    def wait(self):
        for s in (0, 1):
            @pl.when(self.has[s])
            def _():
                self.copies[s].wait_send()
                self.copies[1 - s].wait_recv()


class Sweep:
    def __init__(self, at, half, fx, sx, sxy, ys, yh, zs, zh, sem_x, sem_y, sem_z):
        self.at, self.half, self.fx, self.sx, self.sxy = at, half, fx, sx, sxy
        self.ys, self.yh, self.zs, self.zh = ys, yh, zs, zh
        self.nf, self.bx, self.by, self.bz = half.shape
        bx = self.bx
        self.hx = Halo(at.x, at.nx, lambda x: (x, at.y, at.z),
                       (fx.at[:, 1], fx.at[:, bx]), (fx.at[:, 0], fx.at[:, bx + 1]), sem_x)
        self.hy = Halo(at.y, at.ny, lambda y: (at.x, y, at.z),
                       (ys.at[0], ys.at[1]), (yh.at[0], yh.at[1]), sem_y)
        self.hz = Halo(at.z, at.nz, lambda z: (at.x, at.y, z),
                       (zs.at[0], zs.at[1]), (zh.at[0], zh.at[1]), sem_z)

    def clear_ends(self):
        for s, edge in ((0, 0), (1, self.bx + 1)):
            @pl.when(jnp.logical_not(self.hx.has[s]))
            def _():
                self.fx[:, edge] = jnp.zeros((self.nf, self.by, self.bz), F32)

            @pl.when(jnp.logical_not(self.hy.has[s]))
            def _():
                self.yh[s] = jnp.zeros(self.yh.shape[1:], F32)

            @pl.when(jnp.logical_not(self.hz.has[s]))
            def _():
                self.zh[s] = jnp.zeros(self.zh.shape[1:], F32)

    def start_x(self):
        self.hx.start()

    def x_then_start_y(self):
        self.hx.wait()

        def step(x, _):
            for c in range(self.nf):
                mid = self.fx[c, x + 1]
                s = 0.25 * self.fx[c, x] + 0.5 * mid + 0.25 * self.fx[c, x + 2]
                self.sx[c, x] = s
                row = c * self.bx + x
                self.ys[0, 0, pl.ds(row, 1), :] = mid[0:1]
                self.ys[1, 0, pl.ds(row, 1), :] = mid[self.by - 1:]
                self.ys[0, 1, pl.ds(row, 1), :] = s[0:1]
                self.ys[1, 1, pl.ds(row, 1), :] = s[self.by - 1:]
            return 0

        lax.fori_loop(0, self.bx, step, 0)
        self.hy.start()

    def shift_y(self, tile, c, x, kind):
        sub = lax.broadcasted_iota(jnp.int32, tile.shape, 0)
        row = c * self.bx + x
        lower = jnp.where(sub == 0, self.yh[0, kind, pl.ds(row, 1), :], pltpu.roll(tile, 1, axis=0))
        upper = jnp.where(sub == self.by - 1, self.yh[1, kind, pl.ds(row, 1), :],
                          pltpu.roll(tile, self.by - 1, axis=0))
        return lower, upper

    def y_then_start_z(self):
        self.hy.wait()
        lane = lax.broadcasted_iota(jnp.int32, (self.by, self.zs.shape[2]), 1)
        group = self.nf * self.bx

        def step(x, faces):
            low, high = faces
            for c in range(self.nf):
                tile = self.sx[c, x]
                lower, upper = self.shift_y(tile, c, x, 1)
                s = 0.25 * lower + 0.5 * tile + 0.25 * upper
                self.sxy[c, x] = s
                raw = self.fx[c, x + 1]
                k = c * self.bx + x
                low = jnp.where(lane == k, raw[:, 0:1], low)
                low = jnp.where(lane == k + group, s[:, 0:1], low)
                high = jnp.where(lane == k, raw[:, self.bz - 1:], high)
                high = jnp.where(lane == k + group, s[:, self.bz - 1:], high)
            return low, high

        zero = jnp.zeros(lane.shape, F32)
        low, high = lax.fori_loop(0, self.bx, step, (zero, zero))
        self.zs[0] = low
        self.zs[1] = high
        self.hz.start()

    def finish(self):
        self.hz.wait()
        lane = lax.broadcasted_iota(jnp.int32, (self.by, self.bz), 1)
        width = self.zs.shape[2]
        group = self.nf * self.bx

        def step(x, _):
            turn = lax.rem(width - x, width)
            low, high = (pltpu.roll(self.zh[s], turn, axis=1) for s in (0, 1))

            def shift_z(tile, k):
                lower = jnp.where(lane == 0, low[:, k:k + 1], pltpu.roll(tile, 1, axis=1))
                upper = jnp.where(lane == self.bz - 1, high[:, k:k + 1], pltpu.roll(tile, self.bz - 1, axis=1))
                return lower, upper

            u = [self.fx[c, x + 1] for c in range(3)]
            for c in range(self.nf):
                raw = self.fx[c, x + 1]
                s = self.sxy[c, x]
                lower, upper = shift_z(s, group + c * self.bx)
                smoothed = 0.25 * lower + 0.5 * s + 0.25 * upper
                grad_x = 0.5 * (self.fx[c, x + 2] - self.fx[c, x])
                lower, upper = self.shift_y(raw, c, x, 0)
                grad_y = 0.5 * (upper - lower)
                lower, upper = shift_z(raw, c * self.bx)
                grad_z = 0.5 * (upper - lower)
                self.half[c, x] = smoothed - advection * (u[0] * grad_x + u[1] * grad_y + u[2] * grad_z)
                if c == 3:
                    for v, g in enumerate((grad_x, grad_y, grad_z)):
                        self.half[v, x] = self.half[v, x] - advection * g
            return 0

        lax.fori_loop(0, self.bx, step, 0)


def sweep_scratch(block):
    nf, bx, by, bz = block
    width = -(-2 * nf * bx // 128) * 128
    dma = pltpu.SemaphoreType.DMA((2, 2))
    return [
        pltpu.VMEM((nf, bx + 2, by, bz), F32), pltpu.VMEM(block, F32), pltpu.VMEM(block, F32),
        pltpu.VMEM((2, 2, nf * bx, bz), F32), pltpu.VMEM((2, 2, nf * bx, bz), F32),
        pltpu.VMEM((2, by, width), F32), pltpu.VMEM((2, by, width), F32), dma, dma, dma,
    ]


class Gather:
    def __init__(self, at, piece, line, nodes, sem_l, sem_p):
        self.at, self.piece, self.line, self.nodes, self.sem_l, self.sem_p = at, piece, line, nodes, sem_l, sem_p
        self.on_plane = []

    def start(self):
        at = self.at
        self.on_line = start_all([
            send(self.piece, self.line.at[at.z], self.sem_l, d - 1, at.line_peer(d)[1]) for d in range(1, at.nz)
        ])

    def own(self):
        self.to_plane(0, self.piece, self.at.z)

    def to_plane(self, k, src, z):
        at = self.at
        self.on_plane += start_all([
            send(src, self.nodes.at[at.p, z], self.sem_p, k * (at.plane - 1) + d - 1, at.plane_peer(d)[1])
            for d in range(1, at.plane)
        ])

    def forward(self):
        at = self.at
        for d in range(1, at.nz):
            self.on_line[d - 1].wait_recv()
            z = lax.rem(at.z + at.nz - d, at.nz)
            self.to_plane(d, self.line.at[z], z)
        self.nodes[at.p, at.z] = self.piece[...]
        for d in range(1, at.nz):
            z = lax.rem(at.z + at.nz - d, at.nz)
            self.nodes[at.p, z] = self.line[z]

    def wait(self):
        for c in self.on_line:
            c.wait_send()
        wait_all(self.on_plane)


class Reduce:
    def __init__(self, at, terms, landed_p, sums, landed_l, sem_p, sem_l):
        self.at, self.terms, self.landed_p, self.sums, self.landed_l = at, terms, landed_p, sums, landed_l
        self.sem_p, self.sem_l = sem_p, sem_l
        self.order = list(range(1, at.nz)) + [0]

    def start(self):
        at = self.at
        self.on_plane = {}
        for k in self.order:
            z = lax.rem(at.z + k, at.nz)
            copies = []
            for d in range(1, at.plane):
                p, device = at.plane_peer(d)
                copies.append(send(self.terms.at[p, z], self.landed_p.at[k, d - 1], self.sem_p,
                                   k * (at.plane - 1) + d - 1, device))
            self.on_plane[k] = start_all(copies)

    def forward(self, spread):
        at = self.at
        self.on_line = []
        for k in self.order:
            z = lax.rem(at.z + k, at.nz)
            total = self.terms[at.p, z]
            for d in range(1, at.plane):
                self.on_plane[k][d - 1].wait_recv()
                total = total + self.landed_p[k, d - 1]
            self.sums[k] = total
            for dx in range(spread):
                if k or dx:
                    self.on_line += start_all([
                        send(self.sums.at[k], self.landed_l.at[dx, k], self.sem_l, dx * at.nz + k,
                             at.side_peer(dx, k)[1])
                    ])

    def wait(self):
        wait_all(self.on_line)
        for copies in self.on_plane.values():
            for c in copies:
                c.wait_send()

    def total(self, dx):
        total = self.sums[0] if dx == 0 else self.landed_l[dx, 0]
        for k in range(1, self.at.nz):
            total = total + self.landed_l[dx, k]
        return total


class Couple:
    def __init__(self, sizes, half, nodes, terms, weights_ids, cells, hs, ns, nf32, acc_f, acc_n, speed):
        self.sizes = sizes
        self.half, self.nodes, self.terms = half, nodes, terms
        self.weights_ids, self.cells = weights_ids, cells
        self.hs, self.ns, self.nf32, self.acc_f, self.acc_n, self.speed = hs, ns, nf32, acc_f, acc_n, speed
        self.rows, self.lanes = acc_f.shape[0] // 3, acc_f.shape[1]
        self.size = 3 * self.rows
        self.sources, self.width = cells.shape
        _, self.bx, self.by, self.bz = half.shape
        self.hy = self.by // 2

    def chunks(self, step):
        if self.sources <= 16:
            for q in range(self.sources // 2):
                step(q)
        else:
            pl.loop(0, self.sources // 2)(step)

    def split_store(self, ref, c, value):
        hi = value.astype(BF16)
        ref[c * self.rows:(c + 1) * self.rows] = hi
        ref[self.size + c * self.rows:self.size + (c + 1) * self.rows] = (value - hi.astype(F32)).astype(BF16)

    def pieces(self):
        nx, ny, nz = self.sizes
        pr, pw = self.nodes.shape[3:]
        lp = min(2, nx)
        rp = nx // lp
        for g in range(nx):
            r0, l0 = (g // lp) * pr, (g % lp) * pw
            for y in range(ny):
                for z in range(nz):
                    for c in range(3):
                        r = c * self.rows + (y * nz + z) * (rp * pr) + r0
                        yield g * ny + y, z, c, slice(r, r + pr), slice(l0, l0 + pw)

    def both(self, read, q):
        return jnp.concatenate([read(2 * q), read(2 * q + 1)], axis=1)

    def cell(self, q):
        return self.both(lambda i: self.cells[pl.ds(i, 1), :], q)

    def pair(self, i):
        return self.weights_ids[i], self.weights_ids[i + self.sources]

    def left(self):
        return lax.broadcasted_iota(jnp.int32, (1, self.width), 1) < self.width // 2

    def weight(self, i):
        top, bottom = self.pair(i)
        return jnp.where(self.left(), top, pltpu.roll(bottom, self.width // 2, axis=1))

    def ident(self, i):
        top, bottom = self.pair(i)
        return jnp.where(self.left(), pltpu.roll(top, self.width // 2, axis=1), bottom)

    def cell_place(self, q):
        cell = self.cell(q)
        y = lax.rem(lax.div(cell, self.bz), self.by)
        x = lax.div(cell, self.by * self.bz)
        return self.hots(x * self.hy + lax.rem(y, self.hy), lax.div(y, self.hy) * self.bz + lax.rem(cell, self.bz))

    def node_place(self, q):
        node = self.both(self.ident, q).astype(jnp.int32)
        return self.hots(lax.div(node, self.lanes), lax.rem(node, self.lanes))

    def hots(self, row, lane):
        lane_of = lax.broadcasted_iota(jnp.int32, (self.lanes, 2 * self.width), 0)
        row_of = lax.broadcasted_iota(jnp.int32, (self.rows, 2 * self.width), 0)
        return jnp.where(lane_of == lane, 1.0, 0.0).astype(BF16), row_of == row

    def find(self, ref, hot, mask):
        found = jnp.dot(ref[...], hot, preferred_element_type=F32)
        found = found[:self.size] + found[self.size:]
        return [
            jnp.sum(jnp.where(mask, found[c * self.rows:(c + 1) * self.rows], 0.0), axis=0, keepdims=True)
            for c in range(3)
        ]

    def spread(self, hot, mask, traction, acc):
        high = [t.astype(BF16).astype(F32) for t in traction]
        parts = high + [t - h for t, h in zip(traction, high)]
        values = jnp.concatenate([jnp.where(mask, t, 0.0).astype(BF16) for t in parts], axis=0)
        out = lax.dot_general(values, hot, (((1,), (1,)), ((), ())), preferred_element_type=F32)
        acc[...] += out[:self.size] + out[self.size:]

    def gather_cells(self):
        for c in range(3):
            value = self.half[c]
            top = value[:, :self.hy].reshape(self.rows, self.bz)
            low = value[:, self.hy:].reshape(self.rows, self.bz)
            self.split_store(self.hs, c, jnp.concatenate([top, low], axis=1))
        self.acc_f[...] = jnp.zeros_like(self.acc_f)
        self.acc_n[...] = jnp.zeros_like(self.acc_n)

        def step(q):
            for c, v in enumerate(self.find(self.hs, *self.cell_place(q))):
                self.speed[q, c:c + 1] = v

        self.chunks(step)

    def nodes_to_terms(self):
        for p, z, c, r, l in self.pieces():
            self.nf32[r, l] = self.nodes[p, z, c]
        for c in range(3):
            self.split_store(self.ns, c, self.nf32[c * self.rows:(c + 1) * self.rows])
        total = self.bx * self.by * self.bz

        def step(q):
            factor = jnp.where(self.cell(q) < total, penalty * self.both(self.weight, q), 0.0)
            hot, mask = self.node_place(q)
            shell = self.find(self.ns, hot, mask)
            traction = [factor * (self.speed[q, c:c + 1] - shell[c]) for c in range(3)]
            for c in range(3):
                self.speed[q, c:c + 1] = traction[c]
            self.spread(hot, mask, traction, self.acc_n)

        self.chunks(step)
        for p, z, c, r, l in self.pieces():
            self.terms[p, z, c] = self.acc_n[r, l]

    def force_cells(self, fluid, first):
        def step(q):
            hot, mask = self.cell_place(q)
            self.spread(hot, mask, [self.speed[q, c:c + 1] for c in range(3)], self.acc_f)

        self.chunks(step)
        bx, hy, bz = self.bx, self.hy, self.bz
        for c in range(3):
            force = self.acc_f[c * self.rows:(c + 1) * self.rows]
            fluid[c, first:first + bx, :hy] = self.half[c, :, :hy] - force[:, :bz].reshape(bx, hy, bz)
            fluid[c, first:first + bx, hy:] = self.half[c, :, hy:] - force[:, bz:].reshape(bx, hy, bz)
        fluid[3, first:first + bx] = self.half[3]


def prepare(sizes, shell_raw, weights, elements, owned, counts, shell, rec, cells, joined, total):
    nx, _, nz = sizes
    pr, pw = shell.shape[2:]
    lp = min(2, nx)
    for g in range(nx):
        for r in range(pr):
            m = ((g // lp) * pr + r) * lp * pw + (g % lp) * pw
            for c in range(3):
                shell[g, c, r:r + 1, :] = shell_raw[c:c + 1, m:m + pw]
    ranks, slots = weights.shape[1:]
    joined[:, :slots] = weights[0]
    joined[:, slots:] = elements[0].astype(F32)
    for i in range(ranks):
        rec[i // nz, i % nz] = joined[i:i + 1, :]
    same = lax.broadcasted_iota(jnp.int32, (ranks, ranks), 0) == lax.broadcasted_iota(jnp.int32, (ranks, ranks), 1)
    count = jnp.sum(jnp.where(same, counts[...].astype(F32), 0.0), axis=1, keepdims=True)
    slot = lax.broadcasted_iota(jnp.int32, (ranks, slots), 1).astype(F32)
    value = jnp.where(slot < count, owned[0], total)
    cells[:, :slots] = value[:ranks // 2]
    cells[:, slots:] = value[ranks // 2:]


def whole_kernel(sizes, fluid_in, shell_in, weights_in, elements_in, owned_in, counts_in, fluid, out, *refs):
    refs = list(refs)
    take = lambda n: [refs.pop(0) for _ in range(n)]
    raw = take(5)
    joined, shell, rec, cells, sem_in = take(5)
    line0, line1, nodes0, nodes1, rec_line, records = take(6)
    halves, terms = take(2), take(2)
    reduce0, reduce1 = take(3), take(3)
    mine, last, result = take(3)
    sem_nl0, sem_np0, sem_rl, sem_rp = take(4)
    sem_ap0, sem_al0, sem_nl1, sem_np1, sem_ap1, sem_al1 = take(6)
    couple_refs = take(6)
    sweep_refs = take(10), take(10)
    at = Place(sizes)
    at.greet()
    sweeps = [Sweep(at, h, *r) for h, r in zip(halves, sweep_refs)]
    _, bx, by, bz = halves[0].shape
    pairs = [(fluid_in, sweep_refs[0][0].at[:, 1:bx + 1])]
    pairs += list(zip((shell_in, weights_in, elements_in, owned_in, counts_in), raw))
    fetches = start_all([pltpu.make_async_copy(src, dst, sem_in.at[i]) for i, (src, dst) in enumerate(pairs)])
    for sweep in sweeps:
        sweep.clear_ends()
    wait_all(fetches)
    prepare(sizes, *raw, shell, rec, cells, joined, bx * by * bz)
    at.meet()
    first, second = sweeps
    couples = [Couple(sizes, halves[i], (nodes0, nodes1)[i], terms[i], RecordRows(records), cells, *couple_refs)
               for i in (0, 1)]
    nodes = Gather(at, shell.at[at.x], line0, nodes0, sem_nl0, sem_np0)
    first.start_x()
    rec_copies = []
    for d in range(1, at.nz):
        z, device = at.line_peer(d)
        rec_copies.append(send(rec.at[:, z], rec_line.at[at.z], sem_rl, d - 1, device))
    start_all(rec_copies)
    nodes.start()
    rec_line[at.z] = rec[:, at.z]
    first.x_then_start_y()
    nodes.own()
    wait_all(rec_copies)
    rec_copies = []
    for d in range(1, at.plane):
        p, device = at.plane_peer(d)
        rec_copies.append(send(rec_line.at[:, p], records.at[at.p], sem_rp, d - 1, device))
    start_all(rec_copies)
    nodes.forward()
    records[at.p] = rec_line[:, at.p]
    first.y_then_start_z()
    first.finish()
    couples[0].gather_cells()
    nodes.wait()
    wait_all(rec_copies)
    couples[0].nodes_to_terms()

    loads = Reduce(at, terms[0], *reduce0, sem_ap0, sem_al0)
    loads.start()
    couples[0].force_cells(second.fx, 1)
    second.start_x()
    loads.forward(1)
    second.x_then_start_y()
    loads.wait()
    mine[...] = shell[at.x] + relaxation * loads.total(0)
    nodes = Gather(at, mine, line1, nodes1, sem_nl1, sem_np1)
    nodes.start()
    nodes.own()
    second.y_then_start_z()
    nodes.forward()
    second.finish()
    couples[1].gather_cells()
    nodes.wait()
    couples[1].nodes_to_terms()

    loads = Reduce(at, terms[1], *reduce1, sem_ap1, sem_al1)
    loads.start()
    couples[1].force_cells(result, 0)
    leave = pltpu.make_async_copy(result, fluid, sem_in.at[0])
    leave.start()
    loads.forward(at.nx)
    loads.wait()
    for dx in range(at.nx):
        x = lax.rem(at.x + at.nx - dx, at.nx)
        last[x] = nodes1[x * at.ny + at.y, at.z] + relaxation * loads.total(dx)
    pr, pw = shell.shape[2:]
    lp = min(2, at.nx)
    for g in range(at.nx):
        for r in range(pr):
            m = ((g // lp) * pr + r) * lp * pw + (g % lp) * pw
            for c in range(3):
                out[c:c + 1, m:m + pw] = last[g, c, r:r + 1, :]
    leave.wait()


class RecordRows:
    def __init__(self, records):
        self.records, self.nz = records, records.shape[1]

    def __getitem__(self, i):
        if isinstance(i, int):
            return self.records[i // self.nz, i % self.nz]
        return self.records[lax.div(i, self.nz), lax.rem(i, self.nz)]


def on_device(sizes, fluid_state, shell_disp, quad_weights, quad_elements, owner_cells, owner_counts):
    nx, ny, nz = sizes
    plane = nx * ny
    slots = quad_weights.shape[2]
    ranks = quad_weights.shape[1]
    block = fluid_state.shape
    nodes_here = shell_disp.shape[1]
    lanes = 2 * block[3]
    lp = min(2, nx)
    rp = nx // lp
    pr, pw = nodes_here // lanes // rp, lanes // lp
    piece = (3, pr, pw)
    rec_shape = (plane, nz, 1, 2 * slots)
    shell_shape = (nx,) + piece
    i32 = lambda s: pltpu.VMEM(s, jnp.int32)

    shape = lambda s: jax.ShapeDtypeStruct(s, F32)
    buf = lambda s: pltpu.VMEM(s, F32)
    line = (nz,) + piece
    full = (plane,) + line
    sem = lambda n: pltpu.SemaphoreType.DMA((2, max(n, 1)))
    reduce_scratch = lambda spread: [buf((nz, plane - 1) + piece), buf(line), buf((spread, nz) + piece)]
    rows = ny * nz * rp * pr
    scratch = [
        buf(shell_disp.shape), buf(quad_weights.shape), i32(quad_elements.shape), i32(owner_cells.shape),
        i32(owner_counts.shape),
        buf((ranks, 2 * slots)), buf(shell_shape), buf(rec_shape), i32((ranks // 2, 2 * slots)),
        pltpu.SemaphoreType.DMA((6,)),
        buf(line), buf(line), buf(full), buf(full), buf((nz, plane, 1, 2 * slots)), buf(rec_shape),
        buf(block), buf(block), buf(full), buf(full),
        *reduce_scratch(1), *reduce_scratch(nx), buf(piece), buf(shell_shape), buf(block),
        sem(nz - 1), sem(nz * (plane - 1)), sem(nz - 1), sem(plane - 1),
        sem(nz * (plane - 1)), sem(nz), sem(nz - 1), sem(nz * (plane - 1)), sem(nz * (plane - 1)), sem(nx * nz),
        pltpu.VMEM((6 * rows, lanes), BF16), pltpu.VMEM((6 * rows, lanes), BF16),
        buf((3 * rows, lanes)), buf((3 * rows, lanes)), buf((3 * rows, lanes)), buf((ranks // 4, 3, 4 * slots)),
        *sweep_scratch(block), *sweep_scratch(block),
    ]
    anywhere, vmem = pl.BlockSpec(memory_space=pl.ANY), pl.BlockSpec(memory_space=pltpu.VMEM)
    fluid, out = pl.pallas_call(
        functools.partial(whole_kernel, sizes),
        out_shape=(shape(block), shape(shell_disp.shape)),
        in_specs=[anywhere] * 6, out_specs=(anywhere, vmem),
        scratch_shapes=scratch,
        compiler_params=pltpu.CompilerParams(collective_id=0, has_side_effects=True, vmem_limit_bytes=56 << 20),
    )(fluid_state, shell_disp, quad_weights, quad_elements, owner_cells, owner_counts)
    return fluid, out


def solution(mesh):
    sizes = tuple(mesh.shape[a] for a in AXES)
    return jax.shard_map(
        functools.partial(on_device, sizes),
        mesh=mesh,
        in_specs=(
            P(None, "gx", "gy", "gz"),
            P(None, ("gy", "gz")),
            P(("gx", "gy", "gz"), None, None),
            P(("gx", "gy", "gz"), None, None),
            P(("gx", "gy", "gz"), None, None),
            P(("gx", "gy", "gz"), None),
        ),
        out_specs=(P(None, "gx", "gy", "gz"), P(None, ("gy", "gz"))),
        check_vma=False,
    )
```

profile of v0, /device:TPU:0, one launch (start us, length us, event | category | flops | bytes accessed | tf_op | source)
XLA Modules:
  0.0 58.7 jit_solution(1153150679628196828)
XLA Ops:
  0.6 55.6 %shard_map.77 = (f32[4,16,16,128]{3,2,1,0:T(8,128)}, f32[3,2048]{1,0:T(4,128)}) custom-call(f32[4,16,16,128]{3,2,1,0:T(8,128)} %fluid_in.1, f32[3,2048]{1,0:T(4,128)} %shell_in.1, f32[1,32,64]{2,1,0:T(8,128)} %weights_in.1, s32[1,32,64]{2,1,0:T(8,128)} %elements_in.1, s32[1,32,64]{2,1,0:T(8,128)} %owned_in.1, s32[1,32]{1,0:T(1,128)} %counts_in.1), custom_call_target="tpu_custom_call" | custom-call | tf_op jit(solution)/shard_map/pallas_call | solution.py:606
  56.2 0.0 copy-start
  56.2 1.9 %copy.10 = f32[4,16,16,128]{3,2,1,0:T(8,128)} copy(f32[4,16,16,128]{3,2,1,0:T(8,128)} %get-tuple-element.4) | data formatting | bytes 1048576
  58.1 0.0 copy-done
  58.1 0.6 %copy.11 = f32[3,2048]{1,0:T(4,128)} copy(f32[3,2048]{1,0:T(4,128)S(1)} %copy-done) | data formatting | bytes 49152
Async XLA Ops:
  56.2 1.9 %copy-start = (f32[3,2048]{1,0:T(4,128)S(1)}, f32[3,2048]{1,0:T(4,128)}, u32[]{:S(2)}) copy-start(f32[3,2048]{1,0:T(4,128)} %get-tuple-element.5) | copy-start | bytes 73732
where the time goes:
time: 58.9 us; the launch traced here: 58.7 us
  Pallas kernels  55.6 us (94%)
  local copies, waits for them, and re-layouts  2.49 us (4%)
  between operations  0.65 us (1%)
    pallas_call x1, Pallas kernels, on_device(): pl.pallas_call(functools.partial(whole_kernel, sizes), out_shape=(shape(b...  55.6 us
    unnamed x4, local copies, waits for them, and re-layouts  2.49 us

commit v1 on v0

--- a/solution.py
+++ b/solution.py
@@ -52,9 +52,12 @@
 
 
 def send(src, dst, sems, k, device):
+    return post(src, dst, sems.at[0, k], sems.at[1, k], device)
+
+
+def post(src, dst, send_sem, recv_sem, device):
     return pltpu.make_async_remote_copy(
-        src_ref=src, dst_ref=dst, send_sem=sems.at[0, k], recv_sem=sems.at[1, k],
-        device_id=device, device_id_type=MESH,
+        src_ref=src, dst_ref=dst, send_sem=send_sem, recv_sem=recv_sem, device_id=device, device_id_type=MESH,
     )
 
 
@@ -67,6 +70,10 @@
 def wait_all(copies):
     for c in copies:
         c.wait()
+
+
+def drain(sem, ref):
+    pltpu.make_async_copy(ref, ref, sem).wait()
 
 
 class Halo:
@@ -220,101 +227,101 @@
 
 
 class Gather:
-    def __init__(self, at, piece, line, nodes, sem_l, sem_p):
-        self.at, self.piece, self.line, self.nodes, self.sem_l, self.sem_p = at, piece, line, nodes, sem_l, sem_p
-        self.on_plane = []
+    def __init__(self, at, piece, line, nodes, sem):
+        self.at, self.piece, self.line, self.nodes = at, piece, line, nodes
+        self.line_sent, self.plane_sent, self.plane_here = (sem.at[i] for i in range(3))
+        self.line_here = [sem.at[3 + d] for d in range(at.nz)]
 
     def start(self):
         at = self.at
-        self.on_line = start_all([
-            send(self.piece, self.line.at[at.z], self.sem_l, d - 1, at.line_peer(d)[1]) for d in range(1, at.nz)
-        ])
+        for d in range(1, at.nz):
+            post(self.piece, self.line.at[at.z], self.line_sent, self.line_here[d], at.line_peer(d)[1]).start()
 
     def own(self):
-        self.to_plane(0, self.piece, self.at.z)
-
-    def to_plane(self, k, src, z):
+        self.to_plane(self.piece, self.at.z)
+
+    def to_plane(self, src, z):
         at = self.at
-        self.on_plane += start_all([
-            send(src, self.nodes.at[at.p, z], self.sem_p, k * (at.plane - 1) + d - 1, at.plane_peer(d)[1])
-            for d in range(1, at.plane)
-        ])
+        for d in range(1, at.plane):
+            post(src, self.nodes.at[at.p, z], self.plane_sent, self.plane_here, at.plane_peer(d)[1]).start()
 
     def forward(self):
         at = self.at
         for d in range(1, at.nz):
-            self.on_line[d - 1].wait_recv()
             z = lax.rem(at.z + at.nz - d, at.nz)
-            self.to_plane(d, self.line.at[z], z)
+            drain(self.line_here[d], self.line.at[z])
+            self.to_plane(self.line.at[z], z)
         self.nodes[at.p, at.z] = self.piece[...]
         for d in range(1, at.nz):
             z = lax.rem(at.z + at.nz - d, at.nz)
             self.nodes[at.p, z] = self.line[z]
 
     def wait(self):
-        for c in self.on_line:
-            c.wait_send()
-        wait_all(self.on_plane)
+        at = self.at
+        if at.nz > 1:
+            drain(self.line_sent, self.line.at[:at.nz - 1])
+        if at.plane > 1:
+            drain(self.plane_sent, self.nodes.at[:at.plane - 1])
+            drain(self.plane_here, self.nodes.at[:at.plane - 1])
 
 
 class Reduce:
-    def __init__(self, at, terms, landed_p, sums, landed_l, sem_p, sem_l):
+    def __init__(self, at, terms, landed_p, sums, landed_l, sem):
         self.at, self.terms, self.landed_p, self.sums, self.landed_l = at, terms, landed_p, sums, landed_l
-        self.sem_p, self.sem_l = sem_p, sem_l
+        self.plane_sent, self.line_sent, self.line_here = (sem.at[i] for i in range(3))
+        self.plane_here = [sem.at[3 + k] for k in range(at.nz)]
         self.order = list(range(1, at.nz)) + [0]
 
     def start(self):
         at = self.at
-        self.on_plane = {}
         for k in self.order:
             z = lax.rem(at.z + k, at.nz)
-            copies = []
             for d in range(1, at.plane):
                 p, device = at.plane_peer(d)
-                copies.append(send(self.terms.at[p, z], self.landed_p.at[k, d - 1], self.sem_p,
-                                   k * (at.plane - 1) + d - 1, device))
-            self.on_plane[k] = start_all(copies)
+                post(self.terms.at[p, z], self.landed_p.at[k, d - 1], self.plane_sent, self.plane_here[k],
+                     device).start()
 
     def forward(self, spread):
         at = self.at
-        self.on_line = []
+        self.count = spread * at.nz - 1
         for k in self.order:
             z = lax.rem(at.z + k, at.nz)
             total = self.terms[at.p, z]
+            if at.plane > 1:
+                drain(self.plane_here[k], self.landed_p.at[k])
             for d in range(1, at.plane):
-                self.on_plane[k][d - 1].wait_recv()
                 total = total + self.landed_p[k, d - 1]
             self.sums[k] = total
             for dx in range(spread):
                 if k or dx:
-                    self.on_line += start_all([
-                        send(self.sums.at[k], self.landed_l.at[dx, k], self.sem_l, dx * at.nz + k,
-                             at.side_peer(dx, k)[1])
-                    ])
+                    post(self.sums.at[k], self.landed_l.at[dx * at.nz + k], self.line_sent, self.line_here,
+                         at.side_peer(dx, k)[1]).start()
 
     def wait(self):
-        wait_all(self.on_line)
-        for copies in self.on_plane.values():
-            for c in copies:
-                c.wait_send()
+        if self.count:
+            drain(self.line_sent, self.landed_l.at[1:self.count + 1])
+            drain(self.line_here, self.landed_l.at[1:self.count + 1])
+        if self.at.plane > 1:
+            drain(self.plane_sent, self.landed_p)
 
     def total(self, dx):
-        total = self.sums[0] if dx == 0 else self.landed_l[dx, 0]
-        for k in range(1, self.at.nz):
-            total = total + self.landed_l[dx, k]
+        nz = self.at.nz
+        total = self.sums[0] if dx == 0 else self.landed_l[dx * nz]
+        for k in range(1, nz):
+            total = total + self.landed_l[dx * nz + k]
         return total
 
 
 class Couple:
-    def __init__(self, sizes, half, nodes, terms, weights_ids, cells, hs, ns, nf32, acc_f, acc_n, speed):
+    def __init__(self, sizes, block, cells, records, split, wide, acc_f, acc_n, acc_w, hot_c, hot_n, factor, keep):
         self.sizes = sizes
-        self.half, self.nodes, self.terms = half, nodes, terms
-        self.weights_ids, self.cells = weights_ids, cells
-        self.hs, self.ns, self.nf32, self.acc_f, self.acc_n, self.speed = hs, ns, nf32, acc_f, acc_n, speed
-        self.rows, self.lanes = acc_f.shape[0] // 3, acc_f.shape[1]
+        self.cells, self.records = cells, records
+        self.table, self.wide, self.acc_f, self.acc_n, self.acc_w = split, wide, acc_f, acc_n, acc_w
+        self.hot_c, self.hot_n, self.factor, self.keep = hot_c, hot_n, factor, keep
+        self.rows, self.lanes = acc_w.shape
         self.size = 3 * self.rows
         self.sources, self.width = cells.shape
-        _, self.bx, self.by, self.bz = half.shape
+        _, self.bx, self.by, self.bz = block
         self.hy = self.by // 2
 
     def chunks(self, step):
@@ -324,21 +331,21 @@
         else:
             pl.loop(0, self.sources // 2)(step)
 
-    def split_store(self, ref, c, value):
+    def split_store(self, c, value):
         hi = value.astype(BF16)
-        ref[c * self.rows:(c + 1) * self.rows] = hi
-        ref[self.size + c * self.rows:self.size + (c + 1) * self.rows] = (value - hi.astype(F32)).astype(BF16)
-
-    def pieces(self):
+        self.table[c * self.rows:(c + 1) * self.rows] = hi
+        self.table[self.size + c * self.rows:self.size + (c + 1) * self.rows] = (value - hi.astype(F32)).astype(BF16)
+
+    def pieces(self, nodes):
         nx, ny, nz = self.sizes
-        pr, pw = self.nodes.shape[3:]
+        comps, pr, pw = nodes.shape[2:]
         lp = min(2, nx)
         rp = nx // lp
         for g in range(nx):
             r0, l0 = (g // lp) * pr, (g % lp) * pw
             for y in range(ny):
                 for z in range(nz):
-                    for c in range(3):
+                    for c in range(comps):
                         r = c * self.rows + (y * nz + z) * (rp * pr) + r0
                         yield g * ny + y, z, c, slice(r, r + pr), slice(l0, l0 + pw)
 
@@ -349,7 +356,7 @@
         return self.both(lambda i: self.cells[pl.ds(i, 1), :], q)
 
     def pair(self, i):
-        return self.weights_ids[i], self.weights_ids[i + self.sources]
+        return self.records[i], self.records[i + self.sources]
 
     def left(self):
         return lax.broadcasted_iota(jnp.int32, (1, self.width), 1) < self.width // 2
@@ -362,83 +369,113 @@
         top, bottom = self.pair(i)
         return jnp.where(self.left(), pltpu.roll(top, self.width // 2, axis=1), bottom)
 
+    def hot(self, lane):
+        lane_of = lax.broadcasted_iota(jnp.int32, (self.lanes, 2 * self.width), 0)
+        return jnp.where(lane_of == lane, 1.0, 0.0).astype(BF16)
+
+    def mask(self, row):
+        return lax.broadcasted_iota(jnp.int32, (self.rows, 2 * self.width), 0) == row
+
+    def place_cells(self):
+        def step(q):
+            cell = self.cell(q)
+            y = lax.rem(lax.div(cell, self.bz), self.by)
+            x = lax.div(cell, self.by * self.bz)
+            self.hot_c[q] = self.hot(lax.div(y, self.hy) * self.bz + lax.rem(cell, self.bz))
+            self.keep[q, 0:1] = x * self.hy + lax.rem(y, self.hy)
+
+        self.chunks(step)
+
+    def place_nodes(self):
+        total = self.bx * self.by * self.bz
+
+        def step(q):
+            node = self.both(self.ident, q).astype(jnp.int32)
+            self.hot_n[q] = self.hot(lax.rem(node, self.lanes))
+            self.keep[q, 1:2] = lax.div(node, self.lanes)
+            self.factor[q] = jnp.where(self.cell(q) < total, penalty * self.both(self.weight, q), 0.0)
+
+        self.chunks(step)
+
     def cell_place(self, q):
-        cell = self.cell(q)
-        y = lax.rem(lax.div(cell, self.bz), self.by)
-        x = lax.div(cell, self.by * self.bz)
-        return self.hots(x * self.hy + lax.rem(y, self.hy), lax.div(y, self.hy) * self.bz + lax.rem(cell, self.bz))
+        return self.hot_c[q], self.mask(self.keep[q, 0:1])
 
     def node_place(self, q):
-        node = self.both(self.ident, q).astype(jnp.int32)
-        return self.hots(lax.div(node, self.lanes), lax.rem(node, self.lanes))
-
-    def hots(self, row, lane):
-        lane_of = lax.broadcasted_iota(jnp.int32, (self.lanes, 2 * self.width), 0)
-        row_of = lax.broadcasted_iota(jnp.int32, (self.rows, 2 * self.width), 0)
-        return jnp.where(lane_of == lane, 1.0, 0.0).astype(BF16), row_of == row
-
-    def find(self, ref, hot, mask):
-        found = jnp.dot(ref[...], hot, preferred_element_type=F32)
+        return self.hot_n[q], self.mask(self.keep[q, 1:2])
+
+    def find(self, hot, mask):
+        found = jnp.dot(self.table[...], hot, preferred_element_type=F32)
         found = found[:self.size] + found[self.size:]
         return [
             jnp.sum(jnp.where(mask, found[c * self.rows:(c + 1) * self.rows], 0.0), axis=0, keepdims=True)
             for c in range(3)
         ]
 
-    def spread(self, hot, mask, traction, acc):
-        high = [t.astype(BF16).astype(F32) for t in traction]
-        parts = high + [t - h for t, h in zip(traction, high)]
+    def spread(self, hot, mask, terms, acc):
+        high = [t.astype(BF16).astype(F32) for t in terms]
+        parts = high + [t - h for t, h in zip(terms, high)]
         values = jnp.concatenate([jnp.where(mask, t, 0.0).astype(BF16) for t in parts], axis=0)
         out = lax.dot_general(values, hot, (((1,), (1,)), ((), ())), preferred_element_type=F32)
-        acc[...] += out[:self.size] + out[self.size:]
-
-    def gather_cells(self):
+        n = len(terms) * self.rows
+        acc[:n] += out[:n] + out[n:]
+
+    def weights_to_nodes(self, terms):
+        self.acc_w[...] = jnp.zeros_like(self.acc_w)
+
+        def step(q):
+            hot, mask = self.node_place(q)
+            self.spread(hot, mask, [self.factor[q]], self.acc_w)
+
+        self.chunks(step)
+        for p, z, c, r, l in self.pieces(terms):
+            terms[p, z, c] = self.acc_w[r, l]
+
+    def flow_to_nodes(self, half, terms):
         for c in range(3):
-            value = self.half[c]
+            value = half[c]
             top = value[:, :self.hy].reshape(self.rows, self.bz)
             low = value[:, self.hy:].reshape(self.rows, self.bz)
-            self.split_store(self.hs, c, jnp.concatenate([top, low], axis=1))
+            self.split_store(c, jnp.concatenate([top, low], axis=1))
+        self.acc_n[...] = jnp.zeros_like(self.acc_n)
+
+        def step(q):
+            found = self.find(*self.cell_place(q))
+            hot, mask = self.node_place(q)
+            factor = self.factor[q]
+            self.spread(hot, mask, [factor * v for v in found], self.acc_n)
+
+        self.chunks(step)
+        for p, z, c, r, l in self.pieces(terms):
+            terms[p, z, c] = self.acc_n[r, l]
+
+    def nodes_to_flow(self, nodes, weigh):
+        for p, z, c, r, l in self.pieces(nodes):
+            self.wide[r, l] = nodes[p, z, c]
+        for c in range(3):
+            self.split_store(c, self.wide[c * self.rows:(c + 1) * self.rows])
         self.acc_f[...] = jnp.zeros_like(self.acc_f)
-        self.acc_n[...] = jnp.zeros_like(self.acc_n)
 
         def step(q):
-            for c, v in enumerate(self.find(self.hs, *self.cell_place(q))):
-                self.speed[q, c:c + 1] = v
+            found = self.find(*self.node_place(q))
+            hot, mask = self.cell_place(q)
+            factor = self.factor[q]
+            terms = [factor * s for s in found] + ([factor] if weigh else [])
+            self.spread(hot, mask, terms, self.acc_f)
 
         self.chunks(step)
-
-    def nodes_to_terms(self):
-        for p, z, c, r, l in self.pieces():
-            self.nf32[r, l] = self.nodes[p, z, c]
-        for c in range(3):
-            self.split_store(self.ns, c, self.nf32[c * self.rows:(c + 1) * self.rows])
-        total = self.bx * self.by * self.bz
-
-        def step(q):
-            factor = jnp.where(self.cell(q) < total, penalty * self.both(self.weight, q), 0.0)
-            hot, mask = self.node_place(q)
-            shell = self.find(self.ns, hot, mask)
-            traction = [factor * (self.speed[q, c:c + 1] - shell[c]) for c in range(3)]
-            for c in range(3):
-                self.speed[q, c:c + 1] = traction[c]
-            self.spread(hot, mask, traction, self.acc_n)
-
-        self.chunks(step)
-        for p, z, c, r, l in self.pieces():
-            self.terms[p, z, c] = self.acc_n[r, l]
-
-    def force_cells(self, fluid, first):
-        def step(q):
-            hot, mask = self.cell_place(q)
-            self.spread(hot, mask, [self.speed[q, c:c + 1] for c in range(3)], self.acc_f)
-
-        self.chunks(step)
+        if weigh:
+            self.acc_w[...] = 1.0 - self.acc_f[self.size:]
+
+    def push(self, half, fluid, first):
         bx, hy, bz = self.bx, self.hy, self.bz
+        rest = self.acc_w[...]
         for c in range(3):
             force = self.acc_f[c * self.rows:(c + 1) * self.rows]
-            fluid[c, first:first + bx, :hy] = self.half[c, :, :hy] - force[:, :bz].reshape(bx, hy, bz)
-            fluid[c, first:first + bx, hy:] = self.half[c, :, hy:] - force[:, bz:].reshape(bx, hy, bz)
-        fluid[3, first:first + bx] = self.half[3]
+            for s in (0, 1):
+                y, l = slice(s * hy, (s + 1) * hy), slice(s * bz, (s + 1) * bz)
+                fluid[c, first:first + bx, y] = (
+                    half[c, :, y] * rest[:, l].reshape(bx, hy, bz) + force[:, l].reshape(bx, hy, bz))
+        fluid[3, first:first + bx] = half[3]
 
 
 def prepare(sizes, shell_raw, weights, elements, owned, counts, shell, rec, cells, joined, total):
@@ -469,82 +506,87 @@
     raw = take(5)
     joined, shell, rec, cells, sem_in = take(5)
     line0, line1, nodes0, nodes1, rec_line, records = take(6)
-    halves, terms = take(2), take(2)
-    reduce0, reduce1 = take(3), take(3)
+    half, = take(1)
+    terms0, terms1, terms_w = take(3)
+    reduce0, reduce1, reduce_w = take(3), take(3), take(3)
     mine, last, result = take(3)
-    sem_nl0, sem_np0, sem_rl, sem_rp = take(4)
-    sem_ap0, sem_al0, sem_nl1, sem_np1, sem_ap1, sem_al1 = take(6)
-    couple_refs = take(6)
+    sem_r, sem_g0, sem_g1, sem_a0, sem_a1, sem_aw = take(6)
+    couple_refs = take(9)
     sweep_refs = take(10), take(10)
     at = Place(sizes)
     at.greet()
-    sweeps = [Sweep(at, h, *r) for h, r in zip(halves, sweep_refs)]
-    _, bx, by, bz = halves[0].shape
-    pairs = [(fluid_in, sweep_refs[0][0].at[:, 1:bx + 1])]
-    pairs += list(zip((shell_in, weights_in, elements_in, owned_in, counts_in), raw))
-    fetches = start_all([pltpu.make_async_copy(src, dst, sem_in.at[i]) for i, (src, dst) in enumerate(pairs)])
-    for sweep in sweeps:
+    first, second = [Sweep(at, half, *r) for r in sweep_refs]
+    _, bx, by, bz = half.shape
+    here = sweep_refs[0][0].at[:, 1:bx + 1]
+    fetches = start_all([pltpu.make_async_copy(fluid_in, here, sem_in.at[0])])
+    pairs = list(zip((shell_in, weights_in, elements_in, owned_in, counts_in), raw))
+    fetches += start_all([pltpu.make_async_copy(src, dst, sem_in.at[i + 1]) for i, (src, dst) in enumerate(pairs)])
+    for sweep in (first, second):
         sweep.clear_ends()
     wait_all(fetches)
     prepare(sizes, *raw, shell, rec, cells, joined, bx * by * bz)
     at.meet()
-    first, second = sweeps
-    couples = [Couple(sizes, halves[i], (nodes0, nodes1)[i], terms[i], RecordRows(records), cells, *couple_refs)
-               for i in (0, 1)]
-    nodes = Gather(at, shell.at[at.x], line0, nodes0, sem_nl0, sem_np0)
+    couple = Couple(sizes, half.shape, cells, RecordRows(records), *couple_refs)
+    gather = Gather(at, shell.at[at.x], line0, nodes0, sem_g0)
     first.start_x()
-    rec_copies = []
     for d in range(1, at.nz):
         z, device = at.line_peer(d)
-        rec_copies.append(send(rec.at[:, z], rec_line.at[at.z], sem_rl, d - 1, device))
-    start_all(rec_copies)
-    nodes.start()
+        post(rec.at[:, z], rec_line.at[at.z], sem_r.at[0], sem_r.at[1], device).start()
+    gather.start()
     rec_line[at.z] = rec[:, at.z]
+    couple.place_cells()
     first.x_then_start_y()
-    nodes.own()
-    wait_all(rec_copies)
-    rec_copies = []
+    gather.own()
+    if at.nz > 1:
+        drain(sem_r.at[0], rec_line.at[:at.nz - 1])
+        drain(sem_r.at[1], rec_line.at[:at.nz - 1])
     for d in range(1, at.plane):
         p, device = at.plane_peer(d)
-        rec_copies.append(send(rec_line.at[:, p], records.at[at.p], sem_rp, d - 1, device))
-    start_all(rec_copies)
-    nodes.forward()
+        post(rec_line.at[:, p], records.at[at.p], sem_r.at[2], sem_r.at[3], device).start()
+    gather.forward()
     records[at.p] = rec_line[:, at.p]
     first.y_then_start_z()
+    if at.plane > 1:
+        drain(sem_r.at[2], records.at[:at.plane - 1])
+        drain(sem_r.at[3], records.at[:at.plane - 1])
+    couple.place_nodes()
+    couple.weights_to_nodes(terms_w)
+    weigh = Reduce(at, terms_w, *reduce_w, sem_aw)
+    weigh.start()
     first.finish()
-    couples[0].gather_cells()
-    nodes.wait()
-    wait_all(rec_copies)
-    couples[0].nodes_to_terms()
-
-    loads = Reduce(at, terms[0], *reduce0, sem_ap0, sem_al0)
+    couple.flow_to_nodes(half, terms0)
+    loads = Reduce(at, terms0, *reduce0, sem_a0)
     loads.start()
-    couples[0].force_cells(second.fx, 1)
+    gather.wait()
+    couple.nodes_to_flow(nodes0, True)
+    couple.push(half, second.fx, 1)
     second.start_x()
+    weigh.forward(at.nx)
     loads.forward(1)
     second.x_then_start_y()
+    weigh.wait()
     loads.wait()
-    mine[...] = shell[at.x] + relaxation * loads.total(0)
-    nodes = Gather(at, mine, line1, nodes1, sem_nl1, sem_np1)
-    nodes.start()
-    nodes.own()
+    mine[...] = shell[at.x] * (1.0 - relaxation * weigh.total(0)) + relaxation * loads.total(0)
+    gather = Gather(at, mine, line1, nodes1, sem_g1)
+    gather.start()
+    gather.own()
     second.y_then_start_z()
-    nodes.forward()
+    gather.forward()
     second.finish()
-    couples[1].gather_cells()
-    nodes.wait()
-    couples[1].nodes_to_terms()
-
-    loads = Reduce(at, terms[1], *reduce1, sem_ap1, sem_al1)
+    couple.flow_to_nodes(half, terms1)
+    loads = Reduce(at, terms1, *reduce1, sem_a1)
     loads.start()
-    couples[1].force_cells(result, 0)
+    gather.wait()
+    couple.nodes_to_flow(nodes1, False)
+    couple.push(half, result, 0)
     leave = pltpu.make_async_copy(result, fluid, sem_in.at[0])
     leave.start()
     loads.forward(at.nx)
     loads.wait()
     for dx in range(at.nx):
         x = lax.rem(at.x + at.nx - dx, at.nx)
-        last[x] = nodes1[x * at.ny + at.y, at.z] + relaxation * loads.total(dx)
+        last[x] = (nodes1[x * at.ny + at.y, at.z] * (1.0 - relaxation * weigh.total(dx))
+                   + relaxation * loads.total(dx))
     pr, pw = shell.shape[2:]
     lp = min(2, at.nx)
     for g in range(at.nx):
@@ -585,21 +627,26 @@
     buf = lambda s: pltpu.VMEM(s, F32)
     line = (nz,) + piece
     full = (plane,) + line
-    sem = lambda n: pltpu.SemaphoreType.DMA((2, max(n, 1)))
-    reduce_scratch = lambda spread: [buf((nz, plane - 1) + piece), buf(line), buf((spread, nz) + piece)]
+    thin = (1, pr, pw)
+    sem = lambda n: pltpu.SemaphoreType.DMA((n,))
+
+    def reduce_scratch(spread, item):
+        return [buf((nz, max(plane - 1, 1)) + item), buf((nz,) + item), buf((spread * nz,) + item)]
+
     rows = ny * nz * rp * pr
+    steps = ranks // 4
     scratch = [
         buf(shell_disp.shape), buf(quad_weights.shape), i32(quad_elements.shape), i32(owner_cells.shape),
         i32(owner_counts.shape),
-        buf((ranks, 2 * slots)), buf(shell_shape), buf(rec_shape), i32((ranks // 2, 2 * slots)),
-        pltpu.SemaphoreType.DMA((6,)),
+        buf((ranks, 2 * slots)), buf(shell_shape), buf(rec_shape), i32((ranks // 2, 2 * slots)), sem(6),
         buf(line), buf(line), buf(full), buf(full), buf((nz, plane, 1, 2 * slots)), buf(rec_shape),
-        buf(block), buf(block), buf(full), buf(full),
-        *reduce_scratch(1), *reduce_scratch(nx), buf(piece), buf(shell_shape), buf(block),
-        sem(nz - 1), sem(nz * (plane - 1)), sem(nz - 1), sem(plane - 1),
-        sem(nz * (plane - 1)), sem(nz), sem(nz - 1), sem(nz * (plane - 1)), sem(nz * (plane - 1)), sem(nx * nz),
-        pltpu.VMEM((6 * rows, lanes), BF16), pltpu.VMEM((6 * rows, lanes), BF16),
-        buf((3 * rows, lanes)), buf((3 * rows, lanes)), buf((3 * rows, lanes)), buf((ranks // 4, 3, 4 * slots)),
+        buf(block), buf(full), buf(full), buf((plane, nz) + thin),
+        *reduce_scratch(1, piece), *reduce_scratch(nx, piece), *reduce_scratch(nx, thin),
+        buf(piece), buf(shell_shape), buf(block),
+        sem(4), sem(3 + nz), sem(3 + nz), sem(3 + nz), sem(3 + nz), sem(3 + nz),
+        pltpu.VMEM((6 * rows, lanes), BF16), buf((3 * rows, lanes)), buf((4 * rows, lanes)), buf((3 * rows, lanes)),
+        buf((rows, lanes)), pltpu.VMEM((steps, lanes, 4 * slots), BF16), pltpu.VMEM((steps, lanes, 4 * slots), BF16),
+        buf((steps, 1, 4 * slots)), i32((steps, 2, 4 * slots)),
         *sweep_scratch(block), *sweep_scratch(block),
     ]
     anywhere, vmem = pl.BlockSpec(memory_space=pl.ANY), pl.BlockSpec(memory_space=pltpu.VMEM)

time: 58.9 us -> 53.1 us (0.902)
  Pallas kernels: 55.6 us -> 49.8 us
    pallas_call x1, Pallas kernels: 55.6 us -> 49.8 us  [on_device(): pl.pallas_call(functools.partial(whole_kernel, sizes), out_shape=(shape(b...]
where the time goes in v1:
time: 53.1 us; the launch traced here: 52.9 us
  Pallas kernels  49.8 us (94%)
  local copies, waits for them, and re-layouts  2.49 us (5%)
  between operations  0.65 us (1%)
    pallas_call x1, Pallas kernels, on_device(): pl.pallas_call(functools.partial(whole_kernel, sizes), out_shape=(shape(b...  49.8 us
    unnamed x4, local copies, waits for them, and re-layouts  2.49 us

profile of v1, /device:TPU:0, one launch (start us, length us, event | category | flops | bytes accessed | tf_op | source)
XLA Modules:
  0.0 52.9 jit_solution(8171692220844255591)
XLA Ops:
  0.6 49.8 %shard_map.77 = (f32[4,16,16,128]{3,2,1,0:T(8,128)}, f32[3,2048]{1,0:T(4,128)}) custom-call(f32[4,16,16,128]{3,2,1,0:T(8,128)} %fluid_in.1, f32[3,2048]{1,0:T(4,128)} %shell_in.1, f32[1,32,64]{2,1,0:T(8,128)} %weights_in.1, s32[1,32,64]{2,1,0:T(8,128)} %elements_in.1, s32[1,32,64]{2,1,0:T(8,128)} %owned_in.1, s32[1,32]{1,0:T(1,128)} %counts_in.1), custom_call_target="tpu_custom_call" | custom-call | tf_op jit(solution)/shard_map/pallas_call | solution.py:653
  50.4 0.0 copy-start
  50.4 1.9 %copy.10 = f32[4,16,16,128]{3,2,1,0:T(8,128)} copy(f32[4,16,16,128]{3,2,1,0:T(8,128)} %get-tuple-element.4) | data formatting | bytes 1048576
  52.3 0.0 copy-done
  52.3 0.6 %copy.11 = f32[3,2048]{1,0:T(4,128)} copy(f32[3,2048]{1,0:T(4,128)S(1)} %copy-done) | data formatting | bytes 49152
Async XLA Ops:
  50.4 1.9 %copy-start = (f32[3,2048]{1,0:T(4,128)S(1)}, f32[3,2048]{1,0:T(4,128)}, u32[]{:S(2)}) copy-start(f32[3,2048]{1,0:T(4,128)} %get-tuple-element.5) | copy-start | bytes 73732

commit v2 on v1

--- a/solution.py
+++ b/solution.py
@@ -1,4 +1,6 @@
 import functools
+import itertools
+import math
 
 import jax
 import jax.numpy as jnp
@@ -33,18 +35,37 @@
         z = lax.rem(self.z + d, self.nz)
         return z, (self.x, self.y, z)
 
+    def peers(self):
+        yield from (self.plane_peer(d)[1] for d in range(1, self.plane))
+        for dx in range(self.nx):
+            yield from (self.side_peer(dx, d)[1] for d in range(1, self.nz))
+
+    def corners(self):
+        sizes, place = (self.nx, self.ny, self.nz), (self.x, self.y, self.z)
+        if self.nz > 1 and self.ny > 1:
+            for d in itertools.product((-1, 0, 1), (-1, 1), (-1, 1)):
+                if d[0] and self.nx == 1:
+                    continue
+                there = [p + v for p, v in zip(place, d)]
+                ok = functools.reduce(jnp.logical_and, [
+                    (t >= 0) if v < 0 else (t < n) for t, n, v in zip(there, sizes, d) if v])
+                yield ok, tuple(jnp.clip(t, 0, n - 1) for t, n in zip(there, sizes))
+
     def greet(self):
         sem = pltpu.get_barrier_semaphore()
-        for d in range(1, self.plane):
-            pl.semaphore_signal(sem, inc=1, device_id=self.plane_peer(d)[1], device_id_type=MESH)
-        for d in range(1, self.nz):
-            pl.semaphore_signal(sem, inc=1, device_id=self.line_peer(d)[1], device_id_type=MESH)
-        for dx in range(1, self.nx):
-            for d in range(1, self.nz):
-                pl.semaphore_signal(sem, inc=1, device_id=self.side_peer(dx, d)[1], device_id_type=MESH)
+        for device in self.peers():
+            pl.semaphore_signal(sem, inc=1, device_id=device, device_id_type=MESH)
+        for ok, device in self.corners():
+            @pl.when(ok)
+            def _():
+                pl.semaphore_signal(sem, inc=1, device_id=device, device_id_type=MESH)
 
     def meet(self):
-        pl.semaphore_wait(pltpu.get_barrier_semaphore(), self.plane - 1 + self.nx * (self.nz - 1))
+        sem = pltpu.get_barrier_semaphore()
+        many = self.plane - 1 + self.nx * (self.nz - 1)
+        for ok, _ in self.corners():
+            many += jnp.where(ok, 1, 0)
+        pl.semaphore_wait(sem, many)
 
     def side_peer(self, dx, d):
         x, z = lax.rem(self.x + dx, self.nx), lax.rem(self.z + d, self.nz)
@@ -76,153 +97,161 @@
     pltpu.make_async_copy(ref, ref, sem).wait()
 
 
-class Halo:
-    def __init__(self, here, count, device_of, srcs, dsts, sems):
-        self.has = (here > 0, here < count - 1)
-        self.copies = []
+class Sweep:
+    def __init__(self, at, half, fx, ys, yh, xys, xyh, yb, zs, zh, xzh, yzh, xyzh, sem):
+        self.at, self.half, self.fx, self.ys, self.yh, self.xys, self.xyh, self.yb = at, half, fx, ys, yh, xys, xyh, yb
+        self.zs, self.zh, self.xzh, self.yzh, self.xyzh, self.sem = zs, zh, xzh, yzh, xyzh, sem
+        self.nf, self.bx, self.by, self.bz = half.shape
+        self.place = (at.x, at.y, at.z)
+        self.sizes = (at.nx, at.ny, at.nz)
+        self.kinds = [k for k in itertools.product((0, 1), repeat=3)
+                      if any(k) and all(n > 1 for n, on in zip(self.sizes, k) if on)]
+
+    def clear(self):
+        for edge in (0, self.bx + 1):
+            self.fx[:, edge] = jnp.zeros((self.nf, self.by, self.bz), F32)
+        for ref in (self.yh, self.xys, self.xyh, self.zh, self.xzh, self.yzh, self.xyzh):
+            ref[...] = jnp.zeros(ref.shape, F32)
+
+    def ends(self, kind, d):
+        sx, sy, sz = (int(v > 0) for v in d)
+        bx, by = self.bx, self.by
+        part = self.zs.at[by - 8:by] if sy else self.zs.at[0:8]
+        return {
+            (1, 0, 0): lambda: (self.fx.at[:, bx if sx else 1], self.fx.at[:, 0 if sx else bx + 1]),
+            (0, 1, 0): lambda: (self.ys.at[sy], self.yh.at[1 - sy]),
+            (1, 1, 0): lambda: (self.xys.at[2 * sx + sy], self.xyh.at[2 * (1 - sx) + 1 - sy]),
+            (0, 0, 1): lambda: (self.zs, self.zh.at[1 - sz]),
+            (1, 0, 1): lambda: (self.zs, self.xzh.at[2 * (1 - sx) + 1 - sz]),
+            (0, 1, 1): lambda: (part, self.yzh.at[2 * (1 - sy) + 1 - sz]),
+            (1, 1, 1): lambda: (part, self.xyzh.at[4 * (1 - sx) + 2 * (1 - sy) + 1 - sz]),
+        }[kind]()
+
+    def units(self, kind, n):
+        if kind == (1, 0, 0):
+            return self.fx.at[:, :n]
+        return {
+            (0, 1, 0): self.yh, (1, 1, 0): self.xyh, (0, 0, 1): self.zh,
+            (1, 0, 1): self.xzh, (0, 1, 1): self.yzh, (1, 1, 1): self.xyzh,
+        }[kind].at[:n]
+
+    def start(self, kinds):
+        for kind in kinds:
+            if kind not in self.kinds:
+                continue
+            sems = [self.sem.at[2 * self.kinds.index(kind) + i] for i in (0, 1)]
+            for d in itertools.product(*[(-1, 1) if on else (0,) for on in kind]):
+                there = [p + v for p, v in zip(self.place, d)]
+                ok = functools.reduce(jnp.logical_and, [
+                    (t >= 0) if v < 0 else (t < n) for t, n, v in zip(there, self.sizes, d) if v])
+                device = tuple(jnp.clip(t, 0, n - 1) for t, n in zip(there, self.sizes))
+                src, dst = self.ends(kind, d)
+                copy = post(src, dst, *sems, device)
+
+                @pl.when(ok)
+                def _():
+                    copy.start()
+
+    def wait(self):
+        many = [jnp.where(p > 0, 1, 0) + jnp.where(p < n - 1, 1, 0) for p, n in zip(self.place, self.sizes)]
+        for i, kind in enumerate(self.kinds):
+            counts = [(m, (1,) if n == 2 else (1, 2)) for m, n, on in zip(many, self.sizes, kind) if on]
+            for values in itertools.product(*[c for _, c in counts]):
+                ref = self.units(kind, math.prod(values))
+                ok = functools.reduce(jnp.logical_and, [m == v for (m, _), v in zip(counts, values)])
+
+                @pl.when(ok)
+                def _():
+                    drain(self.sem.at[2 * i], ref)
+                    drain(self.sem.at[2 * i + 1], ref)
+
+    def pack(self):
+        pair = lax.broadcasted_iota(jnp.int32, (self.by, self.bz), 1) // 2
+        face = jnp.zeros((self.by, self.bz), F32)
+        for c in range(self.nf):
+            for x in range(self.bx):
+                k = c * self.bx + x
+                raw = self.fx[c, x + 1]
+                face = jnp.where(pair == k, pltpu.roll(raw, (2 * k + 1) % self.bz, axis=1), face)
+                for s, y in ((0, 0), (1, self.by - 1)):
+                    self.ys[s, k:k + 1] = raw[y:y + 1]
+                    if x in (0, self.bx - 1):
+                        self.xys[2 * int(x > 0) + s, c:c + 1] = raw[y:y + 1]
+        self.zs[...] = face
+
+    def along(self, tile, low, high, axis):
+        at = lax.broadcasted_iota(jnp.int32, tile.shape, axis)
+        n = tile.shape[axis]
+        return (jnp.where(at == 0, low, pltpu.roll(tile, 1, axis=axis)),
+                jnp.where(at == n - 1, high, pltpu.roll(tile, n - 1, axis=axis)))
+
+    def side_lines(self):
         for s in (0, 1):
-            there = jnp.clip(here + (2 * s - 1), 0, count - 1)
-            self.copies.append(send(srcs[s], dsts[1 - s], sems, s, device_of(there)))
-
-    def start(self):
-        for s in (0, 1):
-            @pl.when(self.has[s])
-            def _():
-                self.copies[s].start()
-
-    def wait(self):
-        for s in (0, 1):
-            @pl.when(self.has[s])
-            def _():
-                self.copies[s].wait_send()
-                self.copies[1 - s].wait_recv()
-
-
-class Sweep:
-    def __init__(self, at, half, fx, sx, sxy, ys, yh, zs, zh, sem_x, sem_y, sem_z):
-        self.at, self.half, self.fx, self.sx, self.sxy = at, half, fx, sx, sxy
-        self.ys, self.yh, self.zs, self.zh = ys, yh, zs, zh
-        self.nf, self.bx, self.by, self.bz = half.shape
-        bx = self.bx
-        self.hx = Halo(at.x, at.nx, lambda x: (x, at.y, at.z),
-                       (fx.at[:, 1], fx.at[:, bx]), (fx.at[:, 0], fx.at[:, bx + 1]), sem_x)
-        self.hy = Halo(at.y, at.ny, lambda y: (at.x, y, at.z),
-                       (ys.at[0], ys.at[1]), (yh.at[0], yh.at[1]), sem_y)
-        self.hz = Halo(at.z, at.nz, lambda z: (at.x, at.y, z),
-                       (zs.at[0], zs.at[1]), (zh.at[0], zh.at[1]), sem_z)
-
-    def clear_ends(self):
-        for s, edge in ((0, 0), (1, self.bx + 1)):
-            @pl.when(jnp.logical_not(self.hx.has[s]))
-            def _():
-                self.fx[:, edge] = jnp.zeros((self.nf, self.by, self.bz), F32)
-
-            @pl.when(jnp.logical_not(self.hy.has[s]))
-            def _():
-                self.yh[s] = jnp.zeros(self.yh.shape[1:], F32)
-
-            @pl.when(jnp.logical_not(self.hz.has[s]))
-            def _():
-                self.zh[s] = jnp.zeros(self.zh.shape[1:], F32)
-
-    def start_x(self):
-        self.hx.start()
-
-    def x_then_start_y(self):
-        self.hx.wait()
-
-        def step(x, _):
             for c in range(self.nf):
-                mid = self.fx[c, x + 1]
-                s = 0.25 * self.fx[c, x] + 0.5 * mid + 0.25 * self.fx[c, x + 2]
-                self.sx[c, x] = s
-                row = c * self.bx + x
-                self.ys[0, 0, pl.ds(row, 1), :] = mid[0:1]
-                self.ys[1, 0, pl.ds(row, 1), :] = mid[self.by - 1:]
-                self.ys[0, 1, pl.ds(row, 1), :] = s[0:1]
-                self.ys[1, 1, pl.ds(row, 1), :] = s[self.by - 1:]
-            return 0
-
-        lax.fori_loop(0, self.bx, step, 0)
-        self.hy.start()
-
-    def shift_y(self, tile, c, x, kind):
-        sub = lax.broadcasted_iota(jnp.int32, tile.shape, 0)
-        row = c * self.bx + x
-        lower = jnp.where(sub == 0, self.yh[0, kind, pl.ds(row, 1), :], pltpu.roll(tile, 1, axis=0))
-        upper = jnp.where(sub == self.by - 1, self.yh[1, kind, pl.ds(row, 1), :],
-                          pltpu.roll(tile, self.by - 1, axis=0))
-        return lower, upper
-
-    def y_then_start_z(self):
-        self.hy.wait()
-        lane = lax.broadcasted_iota(jnp.int32, (self.by, self.zs.shape[2]), 1)
-        group = self.nf * self.bx
-
-        def step(x, faces):
-            low, high = faces
-            for c in range(self.nf):
-                tile = self.sx[c, x]
-                lower, upper = self.shift_y(tile, c, x, 1)
-                s = 0.25 * lower + 0.5 * tile + 0.25 * upper
-                self.sxy[c, x] = s
-                raw = self.fx[c, x + 1]
+                rows = slice(c * self.bx, (c + 1) * self.bx)
+                tile = self.yh[s, rows]
+                low, high = self.along(tile, self.xyh[s, c:c + 1], self.xyh[2 + s, c:c + 1], 0)
+                self.yb[s, rows] = (low + high) + (tile + tile)
+
+    def z_faces(self):
+        def thrice(mid, left, right):
+            lane = lax.broadcasted_iota(jnp.int32, mid[0].shape, 1)
+            even = lane % 2 == 0
+            x = (lane // 2) % self.bx
+            mid, left, right = (jnp.where(even, *two) for two in (mid, left, right))
+            w = 2 * (self.bx - 1)
+            low = jnp.where(x == 0, pltpu.roll(left, self.bz - w, axis=1), pltpu.roll(mid, 2, axis=1))
+            high = jnp.where(x == self.bx - 1, pltpu.roll(right, w, axis=1), pltpu.roll(mid, self.bz - 2, axis=1))
+            return mid, (low + high) + (mid + mid)
+
+        def ends(tile):
+            even = lax.broadcasted_iota(jnp.int32, tile.shape, 1) % 2 == 0
+            return jnp.where(even, tile, pltpu.roll(tile, self.bz - 2, axis=1))
+
+        two = lambda ref, i: (ref[i], ref[i + 1])
+        raw, face = thrice(two(self.zh, 0), two(self.xzh, 0), two(self.xzh, 2))
+        _, low = thrice(two(self.yzh, 0), two(self.xyzh, 0), two(self.xyzh, 4))
+        _, high = thrice(two(self.yzh, 2), two(self.xyzh, 2), two(self.xyzh, 6))
+        low, high = self.along(face, low[7:8], high[0:1], 0)
+        return ends(raw), ends((low + high) + (face + face))
+
+    def finish(self):
+        self.side_lines()
+        raw_ends, smooth_ends = self.z_faces()
+        for x in range(self.bx):
+            u = [(0.5 * advection) * self.fx[c, x + 1] for c in range(3)]
+            for c in (3, 0, 1, 2):
                 k = c * self.bx + x
-                low = jnp.where(lane == k, raw[:, 0:1], low)
-                low = jnp.where(lane == k + group, s[:, 0:1], low)
-                high = jnp.where(lane == k, raw[:, self.bz - 1:], high)
-                high = jnp.where(lane == k + group, s[:, self.bz - 1:], high)
-            return low, high
-
-        zero = jnp.zeros(lane.shape, F32)
-        low, high = lax.fori_loop(0, self.bx, step, (zero, zero))
-        self.zs[0] = low
-        self.zs[1] = high
-        self.hz.start()
-
-    def finish(self):
-        self.hz.wait()
-        lane = lax.broadcasted_iota(jnp.int32, (self.by, self.bz), 1)
-        width = self.zs.shape[2]
-        group = self.nf * self.bx
-
-        def step(x, _):
-            turn = lax.rem(width - x, width)
-            low, high = (pltpu.roll(self.zh[s], turn, axis=1) for s in (0, 1))
-
-            def shift_z(tile, k):
-                lower = jnp.where(lane == 0, low[:, k:k + 1], pltpu.roll(tile, 1, axis=1))
-                upper = jnp.where(lane == self.bz - 1, high[:, k:k + 1], pltpu.roll(tile, self.bz - 1, axis=1))
-                return lower, upper
-
-            u = [self.fx[c, x + 1] for c in range(3)]
-            for c in range(self.nf):
-                raw = self.fx[c, x + 1]
-                s = self.sxy[c, x]
-                lower, upper = shift_z(s, group + c * self.bx)
-                smoothed = 0.25 * lower + 0.5 * s + 0.25 * upper
-                grad_x = 0.5 * (self.fx[c, x + 2] - self.fx[c, x])
-                lower, upper = self.shift_y(raw, c, x, 0)
-                grad_y = 0.5 * (upper - lower)
-                lower, upper = shift_z(raw, c * self.bx)
-                grad_z = 0.5 * (upper - lower)
-                self.half[c, x] = smoothed - advection * (u[0] * grad_x + u[1] * grad_y + u[2] * grad_z)
+                below, raw, above = (self.fx[c, x + i] for i in range(3))
+                gx = above - below
+                s = (below + above) + (raw + raw)
+                low, high = self.along(raw, self.yh[0, k:k + 1], self.yh[1, k:k + 1], 0)
+                gy = high - low
+                low, high = self.along(s, self.yb[0, k:k + 1], self.yb[1, k:k + 1], 0)
+                s = (low + high) + (s + s)
+                turn = (self.bz - 2 * k) % self.bz
+                edge = pltpu.roll(raw_ends, turn, axis=1) if turn else raw_ends
+                low, high = self.along(raw, edge, edge, 1)
+                gz = high - low
+                edge = pltpu.roll(smooth_ends, turn, axis=1) if turn else smooth_ends
+                low, high = self.along(s, edge, edge, 1)
+                s = (low + high) + (s + s)
+                new = s * (1.0 / 64.0) - (u[0] * gx + u[1] * gy + u[2] * gz)
                 if c == 3:
-                    for v, g in enumerate((grad_x, grad_y, grad_z)):
-                        self.half[v, x] = self.half[v, x] - advection * g
-            return 0
-
-        lax.fori_loop(0, self.bx, step, 0)
+                    push = [(0.5 * advection) * g for g in (gx, gy, gz)]
+                else:
+                    new = new - push[c]
+                self.half[c, x] = new
 
 
 def sweep_scratch(block):
     nf, bx, by, bz = block
-    width = -(-2 * nf * bx // 128) * 128
-    dma = pltpu.SemaphoreType.DMA((2, 2))
+    rows = nf * bx
+    assert 2 * rows == bz and by >= 8
+    buf = lambda *s: pltpu.VMEM(s, F32)
     return [
-        pltpu.VMEM((nf, bx + 2, by, bz), F32), pltpu.VMEM(block, F32), pltpu.VMEM(block, F32),
-        pltpu.VMEM((2, 2, nf * bx, bz), F32), pltpu.VMEM((2, 2, nf * bx, bz), F32),
-        pltpu.VMEM((2, by, width), F32), pltpu.VMEM((2, by, width), F32), dma, dma, dma,
+        buf(nf, bx + 2, by, bz), buf(2, rows, bz), buf(2, rows, bz), buf(4, 8, bz), buf(4, 8, bz), buf(2, rows, bz),
+        buf(by, bz), buf(2, by, bz), buf(4, by, bz), buf(4, 8, bz), buf(8, 8, bz), pltpu.SemaphoreType.DMA((14,)),
     ]
 
 
@@ -500,6 +529,10 @@
     cells[:, slots:] = value[ranks // 2:]
 
 
+FAR = ((1, 1, 1), (0, 1, 1), (1, 0, 1), (0, 0, 1), (1, 1, 0))
+NEAR = ((0, 1, 0), (1, 0, 0))
+
+
 def whole_kernel(sizes, fluid_in, shell_in, weights_in, elements_in, owned_in, counts_in, fluid, out, *refs):
     refs = list(refs)
     take = lambda n: [refs.pop(0) for _ in range(n)]
@@ -512,40 +545,42 @@
     mine, last, result = take(3)
     sem_r, sem_g0, sem_g1, sem_a0, sem_a1, sem_aw = take(6)
     couple_refs = take(9)
-    sweep_refs = take(10), take(10)
+    sweep_refs = take(12), take(12)
     at = Place(sizes)
+    first, second = [Sweep(at, half, *r) for r in sweep_refs]
+    for sweep in (first, second):
+        sweep.clear()
     at.greet()
-    first, second = [Sweep(at, half, *r) for r in sweep_refs]
     _, bx, by, bz = half.shape
     here = sweep_refs[0][0].at[:, 1:bx + 1]
     fetches = start_all([pltpu.make_async_copy(fluid_in, here, sem_in.at[0])])
     pairs = list(zip((shell_in, weights_in, elements_in, owned_in, counts_in), raw))
     fetches += start_all([pltpu.make_async_copy(src, dst, sem_in.at[i + 1]) for i, (src, dst) in enumerate(pairs)])
-    for sweep in (first, second):
-        sweep.clear_ends()
+    fetches.pop(0).wait()
+    first.pack()
+    at.meet()
+    first.start(FAR + NEAR)
     wait_all(fetches)
     prepare(sizes, *raw, shell, rec, cells, joined, bx * by * bz)
-    at.meet()
     couple = Couple(sizes, half.shape, cells, RecordRows(records), *couple_refs)
     gather = Gather(at, shell.at[at.x], line0, nodes0, sem_g0)
-    first.start_x()
     for d in range(1, at.nz):
         z, device = at.line_peer(d)
         post(rec.at[:, z], rec_line.at[at.z], sem_r.at[0], sem_r.at[1], device).start()
     gather.start()
     rec_line[at.z] = rec[:, at.z]
     couple.place_cells()
-    first.x_then_start_y()
-    gather.own()
     if at.nz > 1:
         drain(sem_r.at[0], rec_line.at[:at.nz - 1])
         drain(sem_r.at[1], rec_line.at[:at.nz - 1])
     for d in range(1, at.plane):
         p, device = at.plane_peer(d)
         post(rec_line.at[:, p], records.at[at.p], sem_r.at[2], sem_r.at[3], device).start()
+    records[at.p] = rec_line[:, at.p]
+    first.wait()
+    gather.own()
     gather.forward()
-    records[at.p] = rec_line[:, at.p]
-    first.y_then_start_z()
+    first.finish()
     if at.plane > 1:
         drain(sem_r.at[2], records.at[:at.plane - 1])
         drain(sem_r.at[3], records.at[:at.plane - 1])
@@ -553,26 +588,25 @@
     couple.weights_to_nodes(terms_w)
     weigh = Reduce(at, terms_w, *reduce_w, sem_aw)
     weigh.start()
-    first.finish()
     couple.flow_to_nodes(half, terms0)
     loads = Reduce(at, terms0, *reduce0, sem_a0)
     loads.start()
     gather.wait()
     couple.nodes_to_flow(nodes0, True)
     couple.push(half, second.fx, 1)
-    second.start_x()
+    second.pack()
+    second.start(FAR + NEAR)
     weigh.forward(at.nx)
     loads.forward(1)
-    second.x_then_start_y()
     weigh.wait()
     loads.wait()
     mine[...] = shell[at.x] * (1.0 - relaxation * weigh.total(0)) + relaxation * loads.total(0)
     gather = Gather(at, mine, line1, nodes1, sem_g1)
     gather.start()
     gather.own()
-    second.y_then_start_z()
+    second.wait()
+    second.finish()
     gather.forward()
-    second.finish()
     couple.flow_to_nodes(half, terms1)
     loads = Reduce(at, terms1, *reduce1, sem_a1)
     loads.start()

time: 53.1 us -> 45.4 us (0.85)
  Pallas kernels: 49.8 us -> 42.1 us
    pallas_call x1, Pallas kernels: 49.8 us -> 42.1 us  [on_device(): pl.pallas_call(functools.partial(whole_kernel, sizes), out_shape=(shape(b...]
where the time goes in v2:
time: 45.4 us; the launch traced here: 45.3 us
  Pallas kernels  42.1 us (93%)
  local copies, waits for them, and re-layouts  2.49 us (5%)
  between operations  0.65 us (1%)
    pallas_call x1, Pallas kernels, on_device(): pl.pallas_call(functools.partial(whole_kernel, sizes), out_shape=(shape(b...  42.1 us
    unnamed x4, local copies, waits for them, and re-layouts  2.49 us

profile of v2, /device:TPU:0, one launch (start us, length us, event | category | flops | bytes accessed | tf_op | source)
XLA Modules:
  0.0 45.3 jit_solution(6772722110998741926)
XLA Ops:
  0.6 42.1 %shard_map.77 = (f32[4,16,16,128]{3,2,1,0:T(8,128)}, f32[3,2048]{1,0:T(4,128)}) custom-call(f32[4,16,16,128]{3,2,1,0:T(8,128)} %fluid_in.1, f32[3,2048]{1,0:T(4,128)} %shell_in.1, f32[1,32,64]{2,1,0:T(8,128)} %weights_in.1, s32[1,32,64]{2,1,0:T(8,128)} %elements_in.1, s32[1,32,64]{2,1,0:T(8,128)} %owned_in.1, s32[1,32]{1,0:T(1,128)} %counts_in.1), custom_call_target="tpu_custom_call" | custom-call | tf_op jit(solution)/shard_map/pallas_call | solution.py:687
  42.8 0.0 copy-start
  42.8 1.9 %copy.10 = f32[4,16,16,128]{3,2,1,0:T(8,128)} copy(f32[4,16,16,128]{3,2,1,0:T(8,128)} %get-tuple-element.4) | data formatting | bytes 1048576
  44.7 0.0 copy-done
  44.7 0.6 %copy.11 = f32[3,2048]{1,0:T(4,128)} copy(f32[3,2048]{1,0:T(4,128)S(1)} %copy-done) | data formatting | bytes 49152
Async XLA Ops:
  42.8 1.9 %copy-start = (f32[3,2048]{1,0:T(4,128)S(1)}, f32[3,2048]{1,0:T(4,128)}, u32[]{:S(2)}) copy-start(f32[3,2048]{1,0:T(4,128)} %get-tuple-element.5) | copy-start | bytes 73732

commit v3 on v2

--- a/solution.py
+++ b/solution.py
@@ -26,6 +26,14 @@
         self.plane = self.nx * self.ny
         self.x, self.y, self.z = (lax.axis_index(a) for a in AXES)
         self.p = self.x * self.ny + self.y
+        assert self.ny % 2 == 0
+        self.half, self.yc, self.par = self.ny // 2, lax.div(self.y, 2), lax.rem(self.y, 2)
+        self.team, self.h = self.nx * self.half, self.x * self.half + self.yc
+        self.mate = (self.x, self.y + 1 - 2 * self.par, self.z)
+
+    def team_peer(self, d):
+        h = lax.rem(self.h + d, self.team)
+        return h, (lax.div(h, self.half), 2 * lax.rem(h, self.half) + self.par, self.z)
 
     def plane_peer(self, d):
         p = lax.rem(self.p + d, self.plane)
@@ -267,31 +275,28 @@
             post(self.piece, self.line.at[at.z], self.line_sent, self.line_here[d], at.line_peer(d)[1]).start()
 
     def own(self):
+        self.nodes[self.at.h, self.at.z] = self.piece[...]
         self.to_plane(self.piece, self.at.z)
 
     def to_plane(self, src, z):
         at = self.at
-        for d in range(1, at.plane):
-            post(src, self.nodes.at[at.p, z], self.plane_sent, self.plane_here, at.plane_peer(d)[1]).start()
-
-    def forward(self):
+        for d in range(1, at.team):
+            post(src, self.nodes.at[at.h, z], self.plane_sent, self.plane_here, at.team_peer(d)[1]).start()
+
+    def forward(self, d):
         at = self.at
-        for d in range(1, at.nz):
-            z = lax.rem(at.z + at.nz - d, at.nz)
-            drain(self.line_here[d], self.line.at[z])
-            self.to_plane(self.line.at[z], z)
-        self.nodes[at.p, at.z] = self.piece[...]
-        for d in range(1, at.nz):
-            z = lax.rem(at.z + at.nz - d, at.nz)
-            self.nodes[at.p, z] = self.line[z]
+        z = lax.rem(at.z + at.nz - d, at.nz)
+        drain(self.line_here[d], self.line.at[z])
+        self.to_plane(self.line.at[z], z)
+        self.nodes[at.h, z] = self.line[z]
 
     def wait(self):
         at = self.at
         if at.nz > 1:
             drain(self.line_sent, self.line.at[:at.nz - 1])
-        if at.plane > 1:
-            drain(self.plane_sent, self.nodes.at[:at.plane - 1])
-            drain(self.plane_here, self.nodes.at[:at.plane - 1])
+        if at.team > 1:
+            drain(self.plane_sent, self.nodes.at[:at.team - 1])
+            drain(self.plane_here, self.nodes.at[:at.team - 1])
 
 
 class Reduce:
@@ -305,8 +310,8 @@
         at = self.at
         for k in self.order:
             z = lax.rem(at.z + k, at.nz)
-            for d in range(1, at.plane):
-                p, device = at.plane_peer(d)
+            for d in range(1, at.team):
+                p, device = at.team_peer(d)
                 post(self.terms.at[p, z], self.landed_p.at[k, d - 1], self.plane_sent, self.plane_here[k],
                      device).start()
 
@@ -315,10 +320,10 @@
         self.count = spread * at.nz - 1
         for k in self.order:
             z = lax.rem(at.z + k, at.nz)
-            total = self.terms[at.p, z]
-            if at.plane > 1:
+            total = self.terms[at.h, z]
+            if at.team > 1:
                 drain(self.plane_here[k], self.landed_p.at[k])
-            for d in range(1, at.plane):
+            for d in range(1, at.team):
                 total = total + self.landed_p[k, d - 1]
             self.sums[k] = total
             for dx in range(spread):
@@ -330,7 +335,7 @@
         if self.count:
             drain(self.line_sent, self.landed_l.at[1:self.count + 1])
             drain(self.line_here, self.landed_l.at[1:self.count + 1])
-        if self.at.plane > 1:
+        if self.at.team > 1:
             drain(self.plane_sent, self.landed_p)
 
     def total(self, dx):
@@ -342,164 +347,193 @@
 
 
 class Couple:
-    def __init__(self, sizes, block, cells, records, split, wide, acc_f, acc_n, acc_w, hot_c, hot_n, factor, keep):
-        self.sizes = sizes
-        self.cells, self.records = cells, records
-        self.table, self.wide, self.acc_f, self.acc_n, self.acc_w = split, wide, acc_f, acc_n, acc_w
-        self.hot_c, self.hot_n, self.factor, self.keep = hot_c, hot_n, factor, keep
-        self.rows, self.lanes = acc_w.shape
-        self.size = 3 * self.rows
-        self.sources, self.width = cells.shape
+    def __init__(self, at, block, cells, records, refs):
+        self.at, self.cells, self.records = at, cells, records
+        (self.table_c, self.table_n, self.wide, self.acc_f, self.acc_n, self.acc_w, self.rest, self.hot_c, self.hot_n,
+         self.factor, self.keep_c, self.keep_n, self.found, self.values) = refs
+        self.rows_c, self.lanes = self.rest.shape
+        self.rows_n = self.acc_w.shape[0]
+        self.sources, self.width = cells.shape[1:]
         _, self.bx, self.by, self.bz = block
         self.hy = self.by // 2
+        self.plain = self.sources <= 16
 
     def chunks(self, step):
-        if self.sources <= 16:
+        if self.plain:
             for q in range(self.sources // 2):
                 step(q)
         else:
             pl.loop(0, self.sources // 2)(step)
 
-    def split_store(self, c, value):
+    def fresh(self, acc):
+        if not self.plain:
+            acc[...] = jnp.zeros_like(acc)
+
+    def split_store(self, table, rows, c, value):
         hi = value.astype(BF16)
-        self.table[c * self.rows:(c + 1) * self.rows] = hi
-        self.table[self.size + c * self.rows:self.size + (c + 1) * self.rows] = (value - hi.astype(F32)).astype(BF16)
+        table[c * rows:(c + 1) * rows] = hi
+        table[(3 + c) * rows:(4 + c) * rows] = (value - hi.astype(F32)).astype(BF16)
 
     def pieces(self, nodes):
-        nx, ny, nz = self.sizes
+        at = self.at
         comps, pr, pw = nodes.shape[2:]
-        lp = min(2, nx)
-        rp = nx // lp
-        for g in range(nx):
+        lp = min(2, at.nx)
+        rp = at.nx // lp
+        for g in range(at.nx):
             r0, l0 = (g // lp) * pr, (g % lp) * pw
-            for y in range(ny):
-                for z in range(nz):
+            for y in range(at.half):
+                for z in range(at.nz):
                     for c in range(comps):
-                        r = c * self.rows + (y * nz + z) * (rp * pr) + r0
-                        yield g * ny + y, z, c, slice(r, r + pr), slice(l0, l0 + pw)
+                        r = c * self.rows_n + (y * at.nz + z) * (rp * pr) + r0
+                        yield g * at.half + y, z, c, slice(r, r + pr), slice(l0, l0 + pw)
 
     def both(self, read, q):
         return jnp.concatenate([read(2 * q), read(2 * q + 1)], axis=1)
 
-    def cell(self, q):
-        return self.both(lambda i: self.cells[pl.ds(i, 1), :], q)
-
-    def pair(self, i):
-        return self.records[i], self.records[i + self.sources]
+    def cell(self, s, q):
+        return self.both(lambda i: self.cells[s, pl.ds(i, 1), :], q)
 
     def left(self):
         return lax.broadcasted_iota(jnp.int32, (1, self.width), 1) < self.width // 2
 
-    def weight(self, i):
-        top, bottom = self.pair(i)
+    def weight(self, s, i):
+        top, bottom = self.records(s, i), self.records(s, i + self.sources)
         return jnp.where(self.left(), top, pltpu.roll(bottom, self.width // 2, axis=1))
 
-    def ident(self, i):
-        top, bottom = self.pair(i)
+    def ident(self, s, i):
+        top, bottom = self.records(s, i), self.records(s, i + self.sources)
         return jnp.where(self.left(), pltpu.roll(top, self.width // 2, axis=1), bottom)
 
     def hot(self, lane):
         lane_of = lax.broadcasted_iota(jnp.int32, (self.lanes, 2 * self.width), 0)
         return jnp.where(lane_of == lane, 1.0, 0.0).astype(BF16)
 
-    def mask(self, row):
-        return lax.broadcasted_iota(jnp.int32, (self.rows, 2 * self.width), 0) == row
-
     def place_cells(self):
         def step(q):
-            cell = self.cell(q)
+            cell = self.cell(0, q)
             y = lax.rem(lax.div(cell, self.bz), self.by)
             x = lax.div(cell, self.by * self.bz)
             self.hot_c[q] = self.hot(lax.div(y, self.hy) * self.bz + lax.rem(cell, self.bz))
-            self.keep[q, 0:1] = x * self.hy + lax.rem(y, self.hy)
+            self.keep_c[q] = x * self.hy + lax.rem(y, self.hy)
 
         self.chunks(step)
 
-    def place_nodes(self):
+    def place_nodes(self, s):
         total = self.bx * self.by * self.bz
+        line = self.rows_n // self.at.half
 
         def step(q):
-            node = self.both(self.ident, q).astype(jnp.int32)
-            self.hot_n[q] = self.hot(lax.rem(node, self.lanes))
-            self.keep[q, 1:2] = lax.div(node, self.lanes)
-            self.factor[q] = jnp.where(self.cell(q) < total, penalty * self.both(self.weight, q), 0.0)
+            node = self.both(lambda i: self.ident(s, i), q).astype(jnp.int32)
+            row = lax.div(node, self.lanes)
+            y = lax.div(row, line)
+            self.hot_n[s, q] = self.hot(lax.rem(node, self.lanes))
+            self.keep_n[s, q] = jnp.where(lax.rem(y, 2) == self.at.par, lax.div(y, 2) * line + lax.rem(row, line), -1)
+            weight = self.both(lambda i: self.weight(s, i), q)
+            self.factor[s, q] = jnp.where(self.cell(s, q) < total, penalty * weight, 0.0)
 
         self.chunks(step)
 
-    def cell_place(self, q):
-        return self.hot_c[q], self.mask(self.keep[q, 0:1])
-
-    def node_place(self, q):
-        return self.hot_n[q], self.mask(self.keep[q, 1:2])
-
-    def find(self, hot, mask):
-        found = jnp.dot(self.table[...], hot, preferred_element_type=F32)
-        found = found[:self.size] + found[self.size:]
+    def find(self, table, rows, hot, row):
+        mask = lax.broadcasted_iota(jnp.int32, (rows, 2 * self.width), 0) == row
+        found = jnp.dot(table[...], hot, preferred_element_type=F32)
+        found = found[:3 * rows] + found[3 * rows:]
         return [
-            jnp.sum(jnp.where(mask, found[c * self.rows:(c + 1) * self.rows], 0.0), axis=0, keepdims=True)
-            for c in range(3)
+            jnp.sum(jnp.where(mask, found[c * rows:(c + 1) * rows], 0.0), axis=0, keepdims=True) for c in range(3)
         ]
 
-    def spread(self, hot, mask, terms, acc):
+    def spread(self, hot, row, terms, acc, rows, first):
+        mask = lax.broadcasted_iota(jnp.int32, (rows, 2 * self.width), 0) == row
         high = [t.astype(BF16).astype(F32) for t in terms]
         parts = high + [t - h for t, h in zip(terms, high)]
         values = jnp.concatenate([jnp.where(mask, t, 0.0).astype(BF16) for t in parts], axis=0)
         out = lax.dot_general(values, hot, (((1,), (1,)), ((), ())), preferred_element_type=F32)
-        n = len(terms) * self.rows
-        acc[:n] += out[:n] + out[n:]
+        n = len(terms) * rows
+        out = out[:n] + out[n:]
+        if first:
+            acc[:n] = out
+        else:
+            acc[:n] += out
+
+    def first(self, q):
+        return self.plain and q == 0
 
     def weights_to_nodes(self, terms):
-        self.acc_w[...] = jnp.zeros_like(self.acc_w)
-
-        def step(q):
-            hot, mask = self.node_place(q)
-            self.spread(hot, mask, [self.factor[q]], self.acc_w)
-
-        self.chunks(step)
+        self.fresh(self.acc_w)
+        for s in (0, 1):
+            self.chunks(lambda q: self.spread(self.hot_n[s, q], self.keep_n[s, q], [self.factor[s, q]], self.acc_w,
+                                              self.rows_n, s == 0 and self.first(q)))
         for p, z, c, r, l in self.pieces(terms):
             terms[p, z, c] = self.acc_w[r, l]
 
-    def flow_to_nodes(self, half, terms):
+    def find_cells(self, half):
         for c in range(3):
             value = half[c]
-            top = value[:, :self.hy].reshape(self.rows, self.bz)
-            low = value[:, self.hy:].reshape(self.rows, self.bz)
-            self.split_store(c, jnp.concatenate([top, low], axis=1))
-        self.acc_n[...] = jnp.zeros_like(self.acc_n)
+            top = value[:, :self.hy].reshape(self.rows_c, self.bz)
+            low = value[:, self.hy:].reshape(self.rows_c, self.bz)
+            self.split_store(self.table_c, self.rows_c, c, jnp.concatenate([top, low], axis=1))
 
         def step(q):
-            found = self.find(*self.cell_place(q))
-            hot, mask = self.node_place(q)
-            factor = self.factor[q]
-            self.spread(hot, mask, [factor * v for v in found], self.acc_n)
+            for c, v in enumerate(self.find(self.table_c, self.rows_c, self.hot_c[q], self.keep_c[q])):
+                self.found[q, c:c + 1] = v
 
         self.chunks(step)
+
+    def swap(self, src, dst, sem):
+        copy = post(src, dst, sem.at[0], sem.at[1], self.at.mate)
+        copy.start()
+        return copy
+
+    def weigh_found(self):
+        def step(q):
+            self.values[0, q] = self.found[q] * self.factor[0, q]
+
+        self.chunks(step)
+
+    def spread_nodes(self, s, incoming):
+        if s == 0:
+            self.fresh(self.acc_n)
+
+        def step(q):
+            terms = [incoming[q, c:c + 1] for c in range(3)]
+            self.spread(self.hot_n[s, q], self.keep_n[s, q], terms, self.acc_n, self.rows_n, s == 0 and self.first(q))
+
+        self.chunks(step)
+
+    def store_terms(self, terms):
         for p, z, c, r, l in self.pieces(terms):
             terms[p, z, c] = self.acc_n[r, l]
 
-    def nodes_to_flow(self, nodes, weigh):
+    def find_nodes(self, s, outgoing):
+        def step(q):
+            for c, v in enumerate(self.find(self.table_n, self.rows_n, self.hot_n[s, q], self.keep_n[s, q])):
+                outgoing[q, c:c + 1] = v
+
+        self.chunks(step)
+
+    def load_nodes(self, nodes):
         for p, z, c, r, l in self.pieces(nodes):
             self.wide[r, l] = nodes[p, z, c]
         for c in range(3):
-            self.split_store(c, self.wide[c * self.rows:(c + 1) * self.rows])
-        self.acc_f[...] = jnp.zeros_like(self.acc_f)
+            self.split_store(self.table_n, self.rows_n, c, self.wide[c * self.rows_n:(c + 1) * self.rows_n])
+
+    def spread_cells(self, incoming, weigh):
+        self.fresh(self.acc_f)
 
         def step(q):
-            found = self.find(*self.node_place(q))
-            hot, mask = self.cell_place(q)
-            factor = self.factor[q]
-            terms = [factor * s for s in found] + ([factor] if weigh else [])
-            self.spread(hot, mask, terms, self.acc_f)
+            factor = self.factor[0, q]
+            terms = [factor * (self.found[q, c:c + 1] + incoming[q, c:c + 1]) for c in range(3)]
+            terms += [factor] if weigh else []
+            self.spread(self.hot_c[q], self.keep_c[q], terms, self.acc_f, self.rows_c, self.first(q))
 
         self.chunks(step)
         if weigh:
-            self.acc_w[...] = 1.0 - self.acc_f[self.size:]
+            self.rest[...] = 1.0 - self.acc_f[3 * self.rows_c:]
 
     def push(self, half, fluid, first):
         bx, hy, bz = self.bx, self.hy, self.bz
-        rest = self.acc_w[...]
+        rest = self.rest[...]
         for c in range(3):
-            force = self.acc_f[c * self.rows:(c + 1) * self.rows]
+            force = self.acc_f[c * self.rows_c:(c + 1) * self.rows_c]
             for s in (0, 1):
                 y, l = slice(s * hy, (s + 1) * hy), slice(s * bz, (s + 1) * bz)
                 fluid[c, first:first + bx, y] = (
@@ -525,8 +559,8 @@
     count = jnp.sum(jnp.where(same, counts[...].astype(F32), 0.0), axis=1, keepdims=True)
     slot = lax.broadcasted_iota(jnp.int32, (ranks, slots), 1).astype(F32)
     value = jnp.where(slot < count, owned[0], total)
-    cells[:, :slots] = value[:ranks // 2]
-    cells[:, slots:] = value[ranks // 2:]
+    cells[0, :, :slots] = value[:ranks // 2]
+    cells[0, :, slots:] = value[ranks // 2:]
 
 
 FAR = ((1, 1, 1), (0, 1, 1), (1, 0, 1), (0, 0, 1), (1, 1, 0))
@@ -543,8 +577,9 @@
     terms0, terms1, terms_w = take(3)
     reduce0, reduce1, reduce_w = take(3), take(3), take(3)
     mine, last, result = take(3)
-    sem_r, sem_g0, sem_g1, sem_a0, sem_a1, sem_aw = take(6)
-    couple_refs = take(9)
+    sem_r, sem_g0, sem_g1, sem_a0, sem_a1, sem_aw, sem_m = take(7)
+    swapped = take(4)
+    couple_refs = take(14)
     sweep_refs = take(12), take(12)
     at = Place(sizes)
     first, second = [Sweep(at, half, *r) for r in sweep_refs]
@@ -562,11 +597,14 @@
     first.start(FAR + NEAR)
     wait_all(fetches)
     prepare(sizes, *raw, shell, rec, cells, joined, bx * by * bz)
-    couple = Couple(sizes, half.shape, cells, RecordRows(records), *couple_refs)
+    sems = [sem_m.at[2 * i:2 * i + 2] for i in range(5)]
+    read = lambda s, i: records[i // at.nz, i % at.nz, at.par if s == 0 else 1 - at.par]
+    couple = Couple(at, half.shape, cells, read, couple_refs)
     gather = Gather(at, shell.at[at.x], line0, nodes0, sem_g0)
     for d in range(1, at.nz):
         z, device = at.line_peer(d)
         post(rec.at[:, z], rec_line.at[at.z], sem_r.at[0], sem_r.at[1], device).start()
+    swaps = [couple.swap(cells.at[0], cells.at[1], sems[0])]
     gather.start()
     rec_line[at.z] = rec[:, at.z]
     couple.place_cells()
@@ -575,24 +613,38 @@
         drain(sem_r.at[1], rec_line.at[:at.nz - 1])
     for d in range(1, at.plane):
         p, device = at.plane_peer(d)
-        post(rec_line.at[:, p], records.at[at.p], sem_r.at[2], sem_r.at[3], device).start()
-    records[at.p] = rec_line[:, at.p]
+        post(rec_line.at[:, pl.ds(2 * lax.div(p, 2), 2)], records.at[at.p], sem_r.at[2], sem_r.at[3], device).start()
+    records[at.p] = rec_line[:, pl.ds(2 * lax.div(at.p, 2), 2)]
     first.wait()
     gather.own()
-    gather.forward()
     first.finish()
-    if at.plane > 1:
-        drain(sem_r.at[2], records.at[:at.plane - 1])
-        drain(sem_r.at[3], records.at[:at.plane - 1])
-    couple.place_nodes()
+    couple.find_cells(half)
+    for d in range(1, at.nz):
+        gather.forward(d)
+    drain(sem_r.at[2], records.at[:at.plane - 1])
+    drain(sem_r.at[3], records.at[:at.plane - 1])
+    couple.place_nodes(0)
+    couple.weigh_found()
+    swaps[0].wait()
+    swaps = [couple.swap(couple.values.at[0], couple.values.at[1], sems[1])]
+    couple.place_nodes(1)
     couple.weights_to_nodes(terms_w)
     weigh = Reduce(at, terms_w, *reduce_w, sem_aw)
     weigh.start()
-    couple.flow_to_nodes(half, terms0)
+    couple.spread_nodes(0, couple.values.at[0])
+    swaps[0].wait()
+    couple.spread_nodes(1, couple.values.at[1])
+    couple.store_terms(terms0)
     loads = Reduce(at, terms0, *reduce0, sem_a0)
     loads.start()
+
     gather.wait()
-    couple.nodes_to_flow(nodes0, True)
+    couple.load_nodes(nodes0)
+    couple.find_nodes(1, swapped[0])
+    swaps = [couple.swap(swapped[0], swapped[1], sems[2])]
+    couple.find_nodes(0, couple.found)
+    swaps[0].wait()
+    couple.spread_cells(swapped[1], True)
     couple.push(half, second.fx, 1)
     second.pack()
     second.start(FAR + NEAR)
@@ -606,12 +658,28 @@
     gather.own()
     second.wait()
     second.finish()
-    gather.forward()
-    couple.flow_to_nodes(half, terms1)
+    couple.find_cells(half)
+    couple.weigh_found()
+    swaps = [couple.swap(couple.values.at[0], couple.values.at[1], sems[3])]
+    if at.nz > 1:
+        gather.forward(1)
+    couple.spread_nodes(0, couple.values.at[0])
+    if at.nz > 2:
+        gather.forward(2)
+    swaps[0].wait()
+    couple.spread_nodes(1, couple.values.at[1])
+    couple.store_terms(terms1)
     loads = Reduce(at, terms1, *reduce1, sem_a1)
     loads.start()
+    for d in range(3, at.nz):
+        gather.forward(d)
     gather.wait()
-    couple.nodes_to_flow(nodes1, False)
+    couple.load_nodes(nodes1)
+    couple.find_nodes(1, swapped[2])
+    swaps = [couple.swap(swapped[2], swapped[3], sems[4])]
+    couple.find_nodes(0, couple.found)
+    swaps[0].wait()
+    couple.spread_cells(swapped[3], False)
     couple.push(half, result, 0)
     leave = pltpu.make_async_copy(result, fluid, sem_in.at[0])
     leave.start()
@@ -619,7 +687,7 @@
     loads.wait()
     for dx in range(at.nx):
         x = lax.rem(at.x + at.nx - dx, at.nx)
-        last[x] = (nodes1[x * at.ny + at.y, at.z] * (1.0 - relaxation * weigh.total(dx))
+        last[x] = (nodes1[x * at.half + at.yc, at.z] * (1.0 - relaxation * weigh.total(dx))
                    + relaxation * loads.total(dx))
     pr, pw = shell.shape[2:]
     lp = min(2, at.nx)
@@ -629,16 +697,6 @@
             for c in range(3):
                 out[c:c + 1, m:m + pw] = last[g, c, r:r + 1, :]
     leave.wait()
-
-
-class RecordRows:
-    def __init__(self, records):
-        self.records, self.nz = records, records.shape[1]
-
-    def __getitem__(self, i):
-        if isinstance(i, int):
-            return self.records[i // self.nz, i % self.nz]
-        return self.records[lax.div(i, self.nz), lax.rem(i, self.nz)]
 
 
 def on_device(sizes, fluid_state, shell_disp, quad_weights, quad_elements, owner_cells, owner_counts):
@@ -660,27 +718,32 @@
     shape = lambda s: jax.ShapeDtypeStruct(s, F32)
     buf = lambda s: pltpu.VMEM(s, F32)
     line = (nz,) + piece
-    full = (plane,) + line
+    team = plane // 2
+    full = (team,) + line
     thin = (1, pr, pw)
     sem = lambda n: pltpu.SemaphoreType.DMA((n,))
 
     def reduce_scratch(spread, item):
-        return [buf((nz, max(plane - 1, 1)) + item), buf((nz,) + item), buf((spread * nz,) + item)]
-
-    rows = ny * nz * rp * pr
-    steps = ranks // 4
+        return [buf((nz, max(team - 1, 1)) + item), buf((nz,) + item), buf((spread * nz,) + item)]
+
+    rows_n = ny * nz * rp * pr // 2
+    rows_c = block[1] * block[2] // 2
+    steps, wide = ranks // 4, 4 * slots
+    half16 = lambda *s: pltpu.VMEM(s, BF16)
     scratch = [
         buf(shell_disp.shape), buf(quad_weights.shape), i32(quad_elements.shape), i32(owner_cells.shape),
         i32(owner_counts.shape),
-        buf((ranks, 2 * slots)), buf(shell_shape), buf(rec_shape), i32((ranks // 2, 2 * slots)), sem(6),
-        buf(line), buf(line), buf(full), buf(full), buf((nz, plane, 1, 2 * slots)), buf(rec_shape),
-        buf(block), buf(full), buf(full), buf((plane, nz) + thin),
+        buf((ranks, 2 * slots)), buf(shell_shape), buf(rec_shape), i32((2, ranks // 2, 2 * slots)), sem(6),
+        buf(line), buf(line), buf(full), buf(full), buf((nz, plane, 1, 2 * slots)), buf((plane, nz, 2, 1, 2 * slots)),
+        buf(block), buf(full), buf(full), buf((team, nz) + thin),
         *reduce_scratch(1, piece), *reduce_scratch(nx, piece), *reduce_scratch(nx, thin),
         buf(piece), buf(shell_shape), buf(block),
-        sem(4), sem(3 + nz), sem(3 + nz), sem(3 + nz), sem(3 + nz), sem(3 + nz),
-        pltpu.VMEM((6 * rows, lanes), BF16), buf((3 * rows, lanes)), buf((4 * rows, lanes)), buf((3 * rows, lanes)),
-        buf((rows, lanes)), pltpu.VMEM((steps, lanes, 4 * slots), BF16), pltpu.VMEM((steps, lanes, 4 * slots), BF16),
-        buf((steps, 1, 4 * slots)), i32((steps, 2, 4 * slots)),
+        sem(4), sem(3 + nz), sem(3 + nz), sem(3 + nz), sem(3 + nz), sem(3 + nz), sem(10),
+        *[buf((steps, 3, wide))] * 4,
+        half16(6 * rows_c, lanes), half16(6 * rows_n, lanes), buf((3 * rows_n, lanes)), buf((4 * rows_c, lanes)),
+        buf((3 * rows_n, lanes)), buf((rows_n, lanes)), buf((rows_c, lanes)),
+        half16(steps, lanes, wide), half16(2, steps, lanes, wide), buf((2, steps, 1, wide)),
+        i32((steps, 1, wide)), i32((2, steps, 1, wide)), buf((steps, 3, wide)), buf((2, steps, 3, wide)),
         *sweep_scratch(block), *sweep_scratch(block),
     ]
     anywhere, vmem = pl.BlockSpec(memory_space=pl.ANY), pl.BlockSpec(memory_space=pltpu.VMEM)

time: 45.4 us -> 47.8 us (1.053)
  Pallas kernels: 42.1 us -> 44.6 us
    pallas_call x1, Pallas kernels: 42.1 us -> 44.6 us  [on_device(): pl.pallas_call(functools.partial(whole_kernel, sizes), out_shape=(shape(b...]
where the time goes in v3:
time: 47.8 us; the launch traced here: 47.7 us
  Pallas kernels  44.6 us (93%)
  local copies, waits for them, and re-layouts  2.49 us (5%)
  between operations  0.65 us (1%)
    pallas_call x1, Pallas kernels, on_device(): pl.pallas_call(functools.partial(whole_kernel, sizes), out_shape=(shape(b...  44.6 us
    unnamed x4, local copies, waits for them, and re-layouts  2.49 us

profile of v3, /device:TPU:0, one launch (start us, length us, event | category | flops | bytes accessed | tf_op | source)
XLA Modules:
  0.0 47.7 jit_solution(5180968133163937578)
XLA Ops:
  0.6 44.6 %shard_map.77 = (f32[4,16,16,128]{3,2,1,0:T(8,128)}, f32[3,2048]{1,0:T(4,128)}) custom-call(f32[4,16,16,128]{3,2,1,0:T(8,128)} %fluid_in.1, f32[3,2048]{1,0:T(4,128)} %shell_in.1, f32[1,32,64]{2,1,0:T(8,128)} %weights_in.1, s32[1,32,64]{2,1,0:T(8,128)} %elements_in.1, s32[1,32,64]{2,1,0:T(8,128)} %owned_in.1, s32[1,32]{1,0:T(1,128)} %counts_in.1), custom_call_target="tpu_custom_call" | custom-call | tf_op jit(solution)/shard_map/pallas_call | solution.py:750
  45.2 0.0 copy-start
  45.2 1.9 %copy.10 = f32[4,16,16,128]{3,2,1,0:T(8,128)} copy(f32[4,16,16,128]{3,2,1,0:T(8,128)} %get-tuple-element.4) | data formatting | bytes 1048576
  47.1 0.0 copy-done
  47.1 0.6 %copy.11 = f32[3,2048]{1,0:T(4,128)} copy(f32[3,2048]{1,0:T(4,128)S(1)} %copy-done) | data formatting | bytes 49152
Async XLA Ops:
  45.2 1.9 %copy-start = (f32[3,2048]{1,0:T(4,128)S(1)}, f32[3,2048]{1,0:T(4,128)}, u32[]{:S(2)}) copy-start(f32[3,2048]{1,0:T(4,128)} %get-tuple-element.5) | copy-start | bytes 73732

commit v4 on v3

--- a/solution.py
+++ b/solution.py
@@ -349,10 +349,10 @@
 class Couple:
     def __init__(self, at, block, cells, records, refs):
         self.at, self.cells, self.records = at, cells, records
-        (self.table_c, self.table_n, self.wide, self.acc_f, self.acc_n, self.acc_w, self.rest, self.hot_c, self.hot_n,
+        (self.table_c, self.table_n, self.wide, self.acc_f, self.acc_n, self.rest, self.hot_c, self.hot_n,
          self.factor, self.keep_c, self.keep_n, self.found, self.values) = refs
         self.rows_c, self.lanes = self.rest.shape
-        self.rows_n = self.acc_w.shape[0]
+        self.rows_n = self.acc_n.shape[0] // 4
         self.sources, self.width = cells.shape[1:]
         _, self.bx, self.by, self.bz = block
         self.hy = self.by // 2
@@ -457,14 +457,6 @@
     def first(self, q):
         return self.plain and q == 0
 
-    def weights_to_nodes(self, terms):
-        self.fresh(self.acc_w)
-        for s in (0, 1):
-            self.chunks(lambda q: self.spread(self.hot_n[s, q], self.keep_n[s, q], [self.factor[s, q]], self.acc_w,
-                                              self.rows_n, s == 0 and self.first(q)))
-        for p, z, c, r, l in self.pieces(terms):
-            terms[p, z, c] = self.acc_w[r, l]
-
     def find_cells(self, half):
         for c in range(3):
             value = half[c]
@@ -489,12 +481,12 @@
 
         self.chunks(step)
 
-    def spread_nodes(self, s, incoming):
+    def spread_nodes(self, s, incoming, weigh):
         if s == 0:
             self.fresh(self.acc_n)
 
         def step(q):
-            terms = [incoming[q, c:c + 1] for c in range(3)]
+            terms = [incoming[q, c:c + 1] for c in range(3)] + ([self.factor[s, q]] if weigh else [])
             self.spread(self.hot_n[s, q], self.keep_n[s, q], terms, self.acc_n, self.rows_n, s == 0 and self.first(q))
 
         self.chunks(step)
@@ -574,12 +566,12 @@
     joined, shell, rec, cells, sem_in = take(5)
     line0, line1, nodes0, nodes1, rec_line, records = take(6)
     half, = take(1)
-    terms0, terms1, terms_w = take(3)
-    reduce0, reduce1, reduce_w = take(3), take(3), take(3)
+    terms0, terms1, ours = take(3)
+    reduce0, reduce1 = take(3), take(3)
     mine, last, result = take(3)
-    sem_r, sem_g0, sem_g1, sem_a0, sem_a1, sem_aw, sem_m = take(7)
+    sem_r, sem_g0, sem_g1, sem_a0, sem_a1, sem_w, sem_m = take(7)
     swapped = take(4)
-    couple_refs = take(14)
+    couple_refs = take(13)
     sweep_refs = take(12), take(12)
     at = Place(sizes)
     first, second = [Sweep(at, half, *r) for r in sweep_refs]
@@ -628,12 +620,9 @@
     swaps[0].wait()
     swaps = [couple.swap(couple.values.at[0], couple.values.at[1], sems[1])]
     couple.place_nodes(1)
-    couple.weights_to_nodes(terms_w)
-    weigh = Reduce(at, terms_w, *reduce_w, sem_aw)
-    weigh.start()
-    couple.spread_nodes(0, couple.values.at[0])
+    couple.spread_nodes(0, couple.values.at[0], True)
     swaps[0].wait()
-    couple.spread_nodes(1, couple.values.at[1])
+    couple.spread_nodes(1, couple.values.at[1], True)
     couple.store_terms(terms0)
     loads = Reduce(at, terms0, *reduce0, sem_a0)
     loads.start()
@@ -648,47 +637,50 @@
     couple.push(half, second.fx, 1)
     second.pack()
     second.start(FAR + NEAR)
-    weigh.forward(at.nx)
     loads.forward(1)
-    weigh.wait()
     loads.wait()
-    mine[...] = shell[at.x] * (1.0 - relaxation * weigh.total(0)) + relaxation * loads.total(0)
+    total = loads.total(0)
+    ours[at.x] = 1.0 - relaxation * total[3:]
+    mine[...] = shell[at.x] * (1.0 - relaxation * total[3:]) + relaxation * total[:3]
     gather = Gather(at, mine, line1, nodes1, sem_g1)
     gather.start()
     gather.own()
+    for dx in range(1, at.nx):
+        device = (lax.rem(at.x + dx, at.nx), at.y, at.z)
+        post(ours.at[at.x], ours.at[at.x], sem_w.at[0], sem_w.at[1], device).start()
     second.wait()
+    if at.nz > 1:
+        gather.forward(1)
     second.finish()
+    for d in range(2, at.nz):
+        gather.forward(d)
     couple.find_cells(half)
     couple.weigh_found()
     swaps = [couple.swap(couple.values.at[0], couple.values.at[1], sems[3])]
-    if at.nz > 1:
-        gather.forward(1)
-    couple.spread_nodes(0, couple.values.at[0])
-    if at.nz > 2:
-        gather.forward(2)
+    couple.spread_nodes(0, couple.values.at[0], False)
     swaps[0].wait()
-    couple.spread_nodes(1, couple.values.at[1])
+    couple.spread_nodes(1, couple.values.at[1], False)
     couple.store_terms(terms1)
     loads = Reduce(at, terms1, *reduce1, sem_a1)
     loads.start()
-    for d in range(3, at.nz):
-        gather.forward(d)
     gather.wait()
     couple.load_nodes(nodes1)
     couple.find_nodes(1, swapped[2])
     swaps = [couple.swap(swapped[2], swapped[3], sems[4])]
     couple.find_nodes(0, couple.found)
+    loads.forward(at.nx)
     swaps[0].wait()
     couple.spread_cells(swapped[3], False)
     couple.push(half, result, 0)
     leave = pltpu.make_async_copy(result, fluid, sem_in.at[0])
     leave.start()
-    loads.forward(at.nx)
+    if at.nx > 1:
+        drain(sem_w.at[0], ours.at[:at.nx - 1])
+        drain(sem_w.at[1], ours.at[:at.nx - 1])
     loads.wait()
     for dx in range(at.nx):
         x = lax.rem(at.x + at.nx - dx, at.nx)
-        last[x] = (nodes1[x * at.half + at.yc, at.z] * (1.0 - relaxation * weigh.total(dx))
-                   + relaxation * loads.total(dx))
+        last[x] = nodes1[x * at.half + at.yc, at.z] * ours[x] + relaxation * loads.total(dx)
     pr, pw = shell.shape[2:]
     lp = min(2, at.nx)
     for g in range(at.nx):
@@ -720,7 +712,7 @@
     line = (nz,) + piece
     team = plane // 2
     full = (team,) + line
-    thin = (1, pr, pw)
+    four, thin = (4, pr, pw), (1, pr, pw)
     sem = lambda n: pltpu.SemaphoreType.DMA((n,))
 
     def reduce_scratch(spread, item):
@@ -735,13 +727,13 @@
         i32(owner_counts.shape),
         buf((ranks, 2 * slots)), buf(shell_shape), buf(rec_shape), i32((2, ranks // 2, 2 * slots)), sem(6),
         buf(line), buf(line), buf(full), buf(full), buf((nz, plane, 1, 2 * slots)), buf((plane, nz, 2, 1, 2 * slots)),
-        buf(block), buf(full), buf(full), buf((team, nz) + thin),
-        *reduce_scratch(1, piece), *reduce_scratch(nx, piece), *reduce_scratch(nx, thin),
+        buf(block), buf((team, nz) + four), buf(full), buf((nx,) + thin),
+        *reduce_scratch(1, four), *reduce_scratch(nx, piece),
         buf(piece), buf(shell_shape), buf(block),
-        sem(4), sem(3 + nz), sem(3 + nz), sem(3 + nz), sem(3 + nz), sem(3 + nz), sem(10),
+        sem(4), sem(3 + nz), sem(3 + nz), sem(3 + nz), sem(3 + nz), sem(2), sem(10),
         *[buf((steps, 3, wide))] * 4,
         half16(6 * rows_c, lanes), half16(6 * rows_n, lanes), buf((3 * rows_n, lanes)), buf((4 * rows_c, lanes)),
-        buf((3 * rows_n, lanes)), buf((rows_n, lanes)), buf((rows_c, lanes)),
+        buf((4 * rows_n, lanes)), buf((rows_c, lanes)),
         half16(steps, lanes, wide), half16(2, steps, lanes, wide), buf((2, steps, 1, wide)),
         i32((steps, 1, wide)), i32((2, steps, 1, wide)), buf((steps, 3, wide)), buf((2, steps, 3, wide)),
         *sweep_scratch(block), *sweep_scratch(block),

time: 47.8 us -> 45.3 us (0.948)
  Pallas kernels: 44.6 us -> 42 us
    pallas_call x1, Pallas kernels: 44.6 us -> 42 us  [on_device(): pl.pallas_call(functools.partial(whole_kernel, sizes), out_shape=(shape(b...]
where the time goes in v4:
time: 45.3 us; the launch traced here: 45.2 us
  Pallas kernels  42 us (93%)
  local copies, waits for them, and re-layouts  2.49 us (5%)
  between operations  0.65 us (1%)
    pallas_call x1, Pallas kernels, on_device(): pl.pallas_call(functools.partial(whole_kernel, sizes), out_shape=(shape(b...  42 us
    unnamed x4, local copies, waits for them, and re-layouts  2.49 us

profile of v4, /device:TPU:0, one launch (start us, length us, event | category | flops | bytes accessed | tf_op | source)
XLA Modules:
  0.0 45.2 jit_solution(18064694917909680898)
XLA Ops:
  0.6 42.0 %shard_map.77 = (f32[4,16,16,128]{3,2,1,0:T(8,128)}, f32[3,2048]{1,0:T(4,128)}) custom-call(f32[4,16,16,128]{3,2,1,0:T(8,128)} %fluid_in.1, f32[3,2048]{1,0:T(4,128)} %shell_in.1, f32[1,32,64]{2,1,0:T(8,128)} %weights_in.1, s32[1,32,64]{2,1,0:T(8,128)} %elements_in.1, s32[1,32,64]{2,1,0:T(8,128)} %owned_in.1, s32[1,32]{1,0:T(1,128)} %counts_in.1), custom_call_target="tpu_custom_call" | custom-call | tf_op jit(solution)/shard_map/pallas_call | solution.py:742
  42.7 0.0 copy-start
  42.7 1.9 %copy.10 = f32[4,16,16,128]{3,2,1,0:T(8,128)} copy(f32[4,16,16,128]{3,2,1,0:T(8,128)} %get-tuple-element.4) | data formatting | bytes 1048576
  44.5 0.0 copy-done
  44.5 0.6 %copy.11 = f32[3,2048]{1,0:T(4,128)} copy(f32[3,2048]{1,0:T(4,128)S(1)} %copy-done) | data formatting | bytes 49152
Async XLA Ops:
  42.7 1.9 %copy-start = (f32[3,2048]{1,0:T(4,128)S(1)}, f32[3,2048]{1,0:T(4,128)}, u32[]{:S(2)}) copy-start(f32[3,2048]{1,0:T(4,128)} %get-tuple-element.5) | copy-start | bytes 73732

commit v5 on v4

--- a/solution.py
+++ b/solution.py
@@ -433,8 +433,23 @@
 
         self.chunks(step)
 
+    def find_all(self, table, rows, hots, keeps, out):
+        def step(j):
+            two = (2 * j, 2 * j + 1)
+            hot = jnp.concatenate([hots[q] for q in two], axis=1)
+            row = jnp.concatenate([keeps[q] for q in two], axis=1)
+            for c, v in enumerate(self.find(table, rows, hot, row)):
+                for i, q in enumerate(two):
+                    out[q, c:c + 1] = v[:, 2 * i * self.width:2 * (i + 1) * self.width]
+
+        if self.plain:
+            for j in range(self.sources // 4):
+                step(j)
+        else:
+            pl.loop(0, self.sources // 4)(step)
+
     def find(self, table, rows, hot, row):
-        mask = lax.broadcasted_iota(jnp.int32, (rows, 2 * self.width), 0) == row
+        mask = lax.broadcasted_iota(jnp.int32, (rows, hot.shape[1]), 0) == row
         found = jnp.dot(table[...], hot, preferred_element_type=F32)
         found = found[:3 * rows] + found[3 * rows:]
         return [
@@ -444,11 +459,16 @@
     def spread(self, hot, row, terms, acc, rows, first):
         mask = lax.broadcasted_iota(jnp.int32, (rows, 2 * self.width), 0) == row
         high = [t.astype(BF16).astype(F32) for t in terms]
-        parts = high + [t - h for t, h in zip(terms, high)]
-        values = jnp.concatenate([jnp.where(mask, t, 0.0).astype(BF16) for t in parts], axis=0)
+        n = len(terms) * rows
+        stack = len(terms) > 3 and rows == self.rows_c
+        high, low = (
+            jnp.concatenate([jnp.where(mask, t, 0.0).astype(BF16) for t in part], axis=0)
+            for part in (high, [t - h for t, h in zip(terms, high)])
+        )
+        values = jnp.concatenate([high, low], axis=int(stack))
+        hot = jnp.concatenate([hot, hot], axis=1) if stack else hot
         out = lax.dot_general(values, hot, (((1,), (1,)), ((), ())), preferred_element_type=F32)
-        n = len(terms) * rows
-        out = out[:n] + out[n:]
+        out = out if stack else out[:n] + out[n:]
         if first:
             acc[:n] = out
         else:
@@ -464,11 +484,7 @@
             low = value[:, self.hy:].reshape(self.rows_c, self.bz)
             self.split_store(self.table_c, self.rows_c, c, jnp.concatenate([top, low], axis=1))
 
-        def step(q):
-            for c, v in enumerate(self.find(self.table_c, self.rows_c, self.hot_c[q], self.keep_c[q])):
-                self.found[q, c:c + 1] = v
-
-        self.chunks(step)
+        self.find_all(self.table_c, self.rows_c, self.hot_c, self.keep_c, self.found)
 
     def swap(self, src, dst, sem):
         copy = post(src, dst, sem.at[0], sem.at[1], self.at.mate)
@@ -496,11 +512,7 @@
             terms[p, z, c] = self.acc_n[r, l]
 
     def find_nodes(self, s, outgoing):
-        def step(q):
-            for c, v in enumerate(self.find(self.table_n, self.rows_n, self.hot_n[s, q], self.keep_n[s, q])):
-                outgoing[q, c:c + 1] = v
-
-        self.chunks(step)
+        self.find_all(self.table_n, self.rows_n, self.hot_n.at[s], self.keep_n.at[s], outgoing)
 
     def load_nodes(self, nodes):
         for p, z, c, r, l in self.pieces(nodes):
@@ -568,7 +580,8 @@
     half, = take(1)
     terms0, terms1, ours = take(3)
     reduce0, reduce1 = take(3), take(3)
-    mine, last, result = take(3)
+    mine, last = take(2)
+    result = fluid
     sem_r, sem_g0, sem_g1, sem_a0, sem_a1, sem_w, sem_m = take(7)
     swapped = take(4)
     couple_refs = take(13)
@@ -638,6 +651,8 @@
     second.pack()
     second.start(FAR + NEAR)
     loads.forward(1)
+    second.wait()
+    second.finish()
     loads.wait()
     total = loads.total(0)
     ours[at.x] = 1.0 - relaxation * total[3:]
@@ -648,18 +663,16 @@
     for dx in range(1, at.nx):
         device = (lax.rem(at.x + dx, at.nx), at.y, at.z)
         post(ours.at[at.x], ours.at[at.x], sem_w.at[0], sem_w.at[1], device).start()
-    second.wait()
-    if at.nz > 1:
-        gather.forward(1)
-    second.finish()
-    for d in range(2, at.nz):
-        gather.forward(d)
     couple.find_cells(half)
     couple.weigh_found()
     swaps = [couple.swap(couple.values.at[0], couple.values.at[1], sems[3])]
     couple.spread_nodes(0, couple.values.at[0], False)
+    if at.nz > 1:
+        gather.forward(1)
     swaps[0].wait()
     couple.spread_nodes(1, couple.values.at[1], False)
+    for d in range(2, at.nz):
+        gather.forward(d)
     couple.store_terms(terms1)
     loads = Reduce(at, terms1, *reduce1, sem_a1)
     loads.start()
@@ -667,13 +680,11 @@
     couple.load_nodes(nodes1)
     couple.find_nodes(1, swapped[2])
     swaps = [couple.swap(swapped[2], swapped[3], sems[4])]
+    loads.forward(at.nx)
     couple.find_nodes(0, couple.found)
-    loads.forward(at.nx)
     swaps[0].wait()
     couple.spread_cells(swapped[3], False)
     couple.push(half, result, 0)
-    leave = pltpu.make_async_copy(result, fluid, sem_in.at[0])
-    leave.start()
     if at.nx > 1:
         drain(sem_w.at[0], ours.at[:at.nx - 1])
         drain(sem_w.at[1], ours.at[:at.nx - 1])
@@ -688,8 +699,6 @@
             m = ((g // lp) * pr + r) * lp * pw + (g % lp) * pw
             for c in range(3):
                 out[c:c + 1, m:m + pw] = last[g, c, r:r + 1, :]
-    leave.wait()
-
 
 def on_device(sizes, fluid_state, shell_disp, quad_weights, quad_elements, owner_cells, owner_counts):
     nx, ny, nz = sizes
@@ -729,7 +738,7 @@
         buf(line), buf(line), buf(full), buf(full), buf((nz, plane, 1, 2 * slots)), buf((plane, nz, 2, 1, 2 * slots)),
         buf(block), buf((team, nz) + four), buf(full), buf((nx,) + thin),
         *reduce_scratch(1, four), *reduce_scratch(nx, piece),
-        buf(piece), buf(shell_shape), buf(block),
+        buf(piece), buf(shell_shape),
         sem(4), sem(3 + nz), sem(3 + nz), sem(3 + nz), sem(3 + nz), sem(2), sem(10),
         *[buf((steps, 3, wide))] * 4,
         half16(6 * rows_c, lanes), half16(6 * rows_n, lanes), buf((3 * rows_n, lanes)), buf((4 * rows_c, lanes)),
@@ -741,8 +750,8 @@
     anywhere, vmem = pl.BlockSpec(memory_space=pl.ANY), pl.BlockSpec(memory_space=pltpu.VMEM)
     fluid, out = pl.pallas_call(
         functools.partial(whole_kernel, sizes),
-        out_shape=(shape(block), shape(shell_disp.shape)),
-        in_specs=[anywhere] * 6, out_specs=(anywhere, vmem),
+        out_shape=(buf(block), buf(shell_disp.shape)),
+        in_specs=[anywhere] * 6, out_specs=(vmem, vmem),
         scratch_shapes=scratch,
         compiler_params=pltpu.CompilerParams(collective_id=0, has_side_effects=True, vmem_limit_bytes=56 << 20),
     )(fluid_state, shell_disp, quad_weights, quad_elements, owner_cells, owner_counts)

time: 45.3 us -> 41.4 us (0.914)
  Pallas kernels: 42 us -> 39.2 us
  local copies, waits for them, and re-layouts: 2.49 us -> 1.41 us
    pallas_call x1, Pallas kernels: 42 us -> 39.2 us  [on_device(): pl.pallas_call(functools.partial(whole_kernel, sizes), out_shape=(buf(blo...]
    unnamed x4 -> x2, local copies, waits for them, and re-layouts: 2.49 us -> 1.41 us
where the time goes in v5:
time: 41.4 us; the launch traced here: 41.3 us
  Pallas kernels  39.2 us (95%)
  local copies, waits for them, and re-layouts  1.41 us (3%)
  between operations  0.64 us (2%)
    pallas_call x1, Pallas kernels, on_device(): pl.pallas_call(functools.partial(whole_kernel, sizes), out_shape=(buf(blo...  39.2 us
    unnamed x2, local copies, waits for them, and re-layouts  1.41 us

profile of v5, /device:TPU:0, one launch (start us, length us, event | category | flops | bytes accessed | tf_op | source)
XLA Modules:
  0.0 41.3 jit_solution(10504084578943122941)
XLA Ops:
  0.6 39.2 %shard_map.77 = (f32[4,16,16,128]{3,2,1,0:T(8,128)S(1)}, f32[3,2048]{1,0:T(4,128)S(1)}) custom-call(f32[4,16,16,128]{3,2,1,0:T(8,128)} %fluid_in.1, f32[3,2048]{1,0:T(4,128)} %shell_in.1, f32[1,32,64]{2,1,0:T(8,128)} %weights_in.1, s32[1,32,64]{2,1,0:T(8,128)} %elements_in.1, s32[1,32,64]{2,1,0:T(8,128)} %owned_in.1, s32[1,32]{1,0:T(1,128)} %counts_in.1), custom_call_target="tpu_custom_call" | custom-call | tf_op jit(solution)/shard_map/pallas_call | solution.py:751
  39.9 0.8 %copy.10 = f32[4,16,16,128]{3,2,1,0:T(8,128)} copy(f32[4,16,16,128]{3,2,1,0:T(8,128)S(1)} %get-tuple-element.2) | data formatting | bytes 1048576
  40.7 0.6 %copy.11 = f32[3,2048]{1,0:T(4,128)} copy(f32[3,2048]{1,0:T(4,128)S(1)} %get-tuple-element.3) | data formatting | bytes 49152

commit v6 on v5

--- a/solution.py
+++ b/solution.py
@@ -667,12 +667,10 @@
     couple.weigh_found()
     swaps = [couple.swap(couple.values.at[0], couple.values.at[1], sems[3])]
     couple.spread_nodes(0, couple.values.at[0], False)
-    if at.nz > 1:
-        gather.forward(1)
+    for d in range(1, at.nz):
+        gather.forward(d)
     swaps[0].wait()
     couple.spread_nodes(1, couple.values.at[1], False)
-    for d in range(2, at.nz):
-        gather.forward(d)
     couple.store_terms(terms1)
     loads = Reduce(at, terms1, *reduce1, sem_a1)
     loads.start()

time: 41.4 us -> 40.6 us (0.981)
  Pallas kernels: 39.2 us -> 38.4 us
    pallas_call x1, Pallas kernels: 39.2 us -> 38.4 us  [on_device(): pl.pallas_call(functools.partial(whole_kernel, sizes), out_shape=(buf(blo...]
where the time goes in v6:
time: 40.6 us; the launch traced here: 40.5 us
  Pallas kernels  38.4 us (95%)
  local copies, waits for them, and re-layouts  1.41 us (3%)
  between operations  0.64 us (2%)
    pallas_call x1, Pallas kernels, on_device(): pl.pallas_call(functools.partial(whole_kernel, sizes), out_shape=(buf(blo...  38.4 us
    unnamed x2, local copies, waits for them, and re-layouts  1.41 us

profile of v6, /device:TPU:0, one launch (start us, length us, event | category | flops | bytes accessed | tf_op | source)
XLA Modules:
  0.0 40.5 jit_solution(12780392431281559055)
XLA Ops:
  0.6 38.4 %shard_map.77 = (f32[4,16,16,128]{3,2,1,0:T(8,128)S(1)}, f32[3,2048]{1,0:T(4,128)S(1)}) custom-call(f32[4,16,16,128]{3,2,1,0:T(8,128)} %fluid_in.1, f32[3,2048]{1,0:T(4,128)} %shell_in.1, f32[1,32,64]{2,1,0:T(8,128)} %weights_in.1, s32[1,32,64]{2,1,0:T(8,128)} %elements_in.1, s32[1,32,64]{2,1,0:T(8,128)} %owned_in.1, s32[1,32]{1,0:T(1,128)} %counts_in.1), custom_call_target="tpu_custom_call" | custom-call | tf_op jit(solution)/shard_map/pallas_call | solution.py:749
  39.0 0.8 %copy.10 = f32[4,16,16,128]{3,2,1,0:T(8,128)} copy(f32[4,16,16,128]{3,2,1,0:T(8,128)S(1)} %get-tuple-element.2) | data formatting | bytes 1048576
  39.8 0.6 %copy.11 = f32[3,2048]{1,0:T(4,128)} copy(f32[3,2048]{1,0:T(4,128)S(1)} %get-tuple-element.3) | data formatting | bytes 49152
